TPU v7x, 512 devices: a whole 4x8x8 slice. The times are simulated.
512 devices in a mesh: apa: 16 (over y, core), wire: 32 (over z, x).
Axes of the slice: x: 4, y: 8, z: 8, core: 2. Of those that a mesh axis runs over, the one named last changes fastest.
Arguments:
- ind_frames: bfloat16 [16, 2, 800, 1024], P('apa', None, 'wire'), may hold values from -6 to 6
- col_frames: bfloat16 [16, 960, 1024], P('apa', 'wire'), may hold values from -6 to 6
- ind_kernel: bfloat16 [2, 11, 256], replicated, may hold values from -0.109375 to 0.109375
- col_kernel: bfloat16 [11, 256], replicated, may hold values from -0.109375 to 0.109375
- cell_u: int32 [16, 32, 512], P('apa', 'wire'), may hold values from 0 to 799
- cell_v: int32 [16, 32, 512], P('apa', 'wire'), may hold values from 0 to 799
- cell_w: int32 [16, 32, 512], P('apa', 'wire'), may hold values from 0 to 959
- tile_counts: int32 [16, 32], P('apa', 'wire'), may hold values from 128 to 512, as said below
Outputs:
- cell_charge: float32 [16, 32, 8, 512], P('apa', 'wire')
Inputs may be any that keep to these rules, and one draw needn't show every extreme that they name: `tile_counts`: each tile holds 512, 256, 170 or 128 live cells, and in every draw some tile holds exactly 512. `cell_u`: slots past a tile's live count also hold wire numbers of the plane.
All inputs are finite; a program needn't handle non-finite values.
Results may differ from a plain program's by a relative error of at most 0.0003.
Values may be sent and summed in bfloat16 or wider, within the bound.
No kernel may reach another device: no remote copies, remote signals or barrier semaphores. Data moves between devices by JAX's collectives and lax.ppermute only.
A program may use at most 64 MiB of HBM per device.

v0:
```python
import jax
import jax.numpy as jnp
from jax import lax
from jax.sharding import PartitionSpec as P

BLOCK = 128


def extended(cells, sides, width):
    for axis, dim in sides:
        count = lax.axis_size(axis)
        ends = count - 1
        head = lax.slice_in_dim(cells, 0, width, axis=dim)
        tail = lax.slice_in_dim(cells, cells.shape[dim] - width, cells.shape[dim], axis=dim)
        cells = jnp.concatenate(
            [
                lax.ppermute(tail, axis, [(i, (i + 1) % count) for i in range(ends)]),
                cells,
                lax.ppermute(head, axis, [((i + 1) % count, i) for i in range(ends)]),
            ],
            axis=dim,
        )
    return cells


def block_matrices(kernel, block_len):
    tap_count = kernel.shape[-1]
    lag_count = tap_count // block_len + 1
    lead = kernel.shape[:-1]
    padded = jnp.pad(kernel, [(0, 0)] * (kernel.ndim - 1) + [(block_len, block_len + 1)])
    full_len = padded.shape[-1]
    tiled = jnp.tile(padded, [1] * (kernel.ndim - 1) + [block_len])
    tiled = tiled[..., : block_len * (full_len - 1)]
    skewed = tiled.reshape(lead + (block_len, full_len - 1))
    kept = skewed[..., block_len : block_len + lag_count * block_len]
    kept = kept.reshape(lead + (block_len, lag_count, block_len))
    axis_count = len(lead)
    order = tuple(range(axis_count)) + (axis_count + 1, axis_count, axis_count + 2)
    return jnp.transpose(kept, order)


def deconvolve(padded, matrices, block_len):
    apa_count, plane_count, wide_count, tick_count = padded.shape
    tap_total = matrices.shape[1]
    lag_count = matrices.shape[2]
    history = lag_count - 1
    wire_count = wide_count - (tap_total - 1)
    block_count = tick_count // block_len
    shifted = jnp.pad(padded, ((0, 0), (0, 0), (0, 0), (history * block_len, 0)))
    blocked = shifted.reshape(apa_count, plane_count, wide_count, block_count + history, block_len)
    summed = jnp.zeros((apa_count, plane_count, wire_count, block_count, block_len), jnp.float32)
    for offset in range(tap_total):
        for lag in range(lag_count):
            source = blocked[
                :, :, offset : offset + wire_count, history - lag : history - lag + block_count
            ]
            summed = summed + jnp.einsum(
                "apwbr,pro->apwbo",
                source,
                matrices[:, offset, lag],
                preferred_element_type=jnp.float32,
            )
    return summed.reshape(apa_count, plane_count, wire_count, tick_count)


def prepare(cleaned):
    apa_count, row_count, tick_count = cleaned.shape
    return cleaned.reshape(apa_count, row_count, tick_count // 4, 4).sum(axis=-1)


def lookup(table, index):
    apa_count, row_count, bin_count = table.shape
    wanted = index[:, 0, :]
    spread = jnp.broadcast_to(wanted[:, :, None], (apa_count, wanted.shape[1], bin_count))
    picked = jnp.take_along_axis(table, spread, axis=1)
    return jnp.transpose(picked, (0, 2, 1))


def on_device(ind_frames, col_frames, ind_kernel, col_kernel, cell_u, cell_v, cell_w, tile_counts):
    block_len = BLOCK
    wire_reach = (ind_kernel.shape[1] - 1) // 2
    apa_count = ind_frames.shape[0]
    ind_width = ind_frames.shape[2]
    col_width = col_frames.shape[1]
    tick_count = ind_frames.shape[3]
    ind_matrices = block_matrices(ind_kernel, block_len)
    col_matrices = block_matrices(col_kernel[None], block_len)
    ind_wide = extended(ind_frames, (("wire", 2),), wire_reach)
    col_wide = extended(col_frames, (("wire", 1),), wire_reach)
    ind_clean = deconvolve(ind_wide, ind_matrices, block_len).reshape(
        apa_count, 2 * ind_width, tick_count
    )
    col_clean = deconvolve(col_wide[:, None], col_matrices, block_len)[:, 0]
    outgoing = jnp.concatenate([prepare(ind_clean), prepare(col_clean)], axis=1)
    gathered = lax.all_to_all(outgoing, "wire", split_axis=2, concat_axis=1, tiled=True)
    unit_size = 2 * ind_width + col_width
    first_slot = cell_u // ind_width * unit_size + cell_u % ind_width
    second_slot = cell_v // ind_width * unit_size + ind_width + cell_v % ind_width
    third_slot = cell_w // col_width * unit_size + 2 * ind_width + cell_w % col_width
    charge = jnp.minimum(
        jnp.minimum(lookup(gathered, first_slot), lookup(gathered, second_slot)),
        lookup(gathered, third_slot),
    )
    live = jnp.arange(cell_u.shape[2], dtype=jnp.int32)[None, None, :] < tile_counts[:, :, None]
    charge = jnp.where(live, charge, jnp.zeros_like(charge))
    return charge[:, None]


def solution(mesh):
    return jax.shard_map(
        on_device,
        mesh=mesh,
        in_specs=(
            P("apa", None, "wire", None),
            P("apa", "wire", None),
            P(),
            P(),
            P("apa", "wire", None),
            P("apa", "wire", None),
            P("apa", "wire", None),
            P("apa", "wire"),
        ),
        out_specs=P("apa", "wire", None, None),
        check_vma=False,
    )
```

profile of v0, /device:TPU:56, one launch (start us, length us, event | category | flops | bytes accessed | tf_op | source)
XLA Modules:
  0.0 197.4 jit_solution(11454938278035215169)
XLA Ops:
  0.0 0.8 fusion.66
  0.8 3.4 %collective-permute-start = (bf16[1,2,5,1024]{3,1,2,0:T(2,128)(2,1)S(1)}, bf16[1,2,5,1024]{3,1,2,0:T(2,128)(2,1)S(1)}, u32[]{:S(2)}, u32[]{:S(2)}) collective-permute-start(bf16[1,2,5,1024]{3,1,2,0:T(2,128)(2,1)S(1)} %get-tuple-element.72), channel_id=1, source_target_pairs={{0,1},{1,2},{2,3},{3,4},{4,5},{5,6},{6,7},{7,8},{8,9},{9,10},{10,1... | collective-permute-start | bytes 61448 | tf_op jit(solution)/shard_map/ppermute | solution.py:17
  4.2 1.3 collective-permute-start.1
  5.5 1.4 fusion.67
  6.8 5.1 %collective-permute-start.2 = (bf16[1,5,1024]{2,1,0:T(8,128)(2,1)}, bf16[1,5,1024]{2,1,0:T(8,128)(2,1)}, u32[]{:S(2)}, u32[]{:S(2)}) collective-permute-start(bf16[1,5,1024]{2,1,0:T(8,128)(2,1)} %get-tuple-element.74), channel_id=1, source_target_pairs={{0,1},{1,2},{2,3},{3,4},{4,5},{5,6},{6,7},{7,8},{8,9},{9,10},{10,1... | collective-permute-start | bytes 30728 | tf_op jit(solution)/shard_map/ppermute | solution.py:17
  12.0 1.3 collective-permute-start.3
  13.3 0.7 pad_bitcast_fusion
  14.0 1.4 tile.23
  15.4 5.0 %tile.24 = bf16[1,11,65664]{2,1,0:T(8,128)(2,1)S(1)} reshape(bf16[11,128,513]{2,1,0:T(8,128)(2,1)} %tile.23) | data formatting | bytes 2889216 | tf_op jit(solution)/shard_map/tile | solution.py:32
  20.5 0.7 copy.266
  21.2 1.3 slice_bitcast_fusion
  23.4 0.3 fusion.46
  23.7 0.3 fusion.43
  24.0 0.6 iota_compare_fusion.1
  24.6 2.0 %tile.20 = bf16[2,11,128,513]{3,2,0,1:T(8,128)(2,1)} broadcast(bf16[2,11,513]{2,0,1:T(2,128)(2,1)S(1)} %pad.16), dimensions={0,1,3} | broadcast | bytes 2911788 | tf_op jit(solution)/shard_map/tile | solution.py:32
  26.7 11.2 %tile.21 = bf16[2,11,65664]{2,0,1:T(2,128)(2,1)S(1)} reshape(bf16[2,11,128,513]{3,2,0,1:T(8,128)(2,1)} %tile.20) | data formatting | bytes 5778432 | tf_op jit(solution)/shard_map/tile | solution.py:32
  37.9 4.0 %slice.566 = bf16[2,11,65536]{2,0,1:T(2,128)(2,1)} slice(bf16[2,11,65664]{2,0,1:T(2,128)(2,1)S(1)} %tile.21), slice={[0:2], [0:11], [0:65536]} | slice | bytes 5767168 | tf_op jit(solution)/shard_map/slice | solution.py:33
  41.9 6.9 %reshape.468 = bf16[2,11,128,512]{3,2,0,1:T(8,128)(2,1)S(1)} reshape(bf16[2,11,65536]{2,0,1:T(2,128)(2,1)} %slice.566) | data formatting | bytes 5767168 | tf_op jit(solution)/shard_map/reshape | solution.py:34
  48.9 1.6 slice.567
  50.5 4.1 %copy.87 = bf16[2,11,128,384]{2,3,1,0:T(8,128)(2,1)} copy(bf16[2,11,128,384]{3,2,0,1:T(8,128)(2,1)} %slice.567) | data formatting | bytes 4325376 | tf_op jit(solution)/shard_map/slice | solution.py:35
  54.7 3.0 %copy.88 = bf16[2,11,128,3,128]{4,2,0,3,1:T(8,128)(2,1)S(1)} copy(bf16[2,11,128,3,128]{2,4,3,1,0:T(8,128)(2,1)} %bitcast.911) | data formatting | bytes 4325376 | tf_op jit(solution)/shard_map/reshape | solution.py:36
  57.6 2.3 %slice.635 = bf16[1,11,128,384]{3,2,1,0:T(8,128)(2,1)} slice(bf16[1,11,128,512]{3,2,1,0:T(8,128)(2,1)} %slice_bitcast_fusion), slice={[0:1], [0:11], [0:128], [128:512]} | slice | bytes 2162688 | tf_op jit(solution)/shard_map/slice | solution.py:35
  60.0 2.4 %copy.232 = bf16[1,11,128,384]{2,3,1,0:T(8,128)(2,1)} copy(bf16[1,11,128,384]{3,2,1,0:T(8,128)(2,1)} %slice.635) | data formatting | bytes 2162688
  62.3 2.4 %copy.124 = bf16[1,11,128,3,128]{4,2,3,1,0:T(8,128)(2,1)} copy(bf16[1,11,128,3,128]{2,4,3,1,0:T(8,128)(2,1)} %bitcast.947) | data formatting | bytes 2162688 | tf_op jit(solution)/shard_map/reshape | solution.py:36
  65.0 0.8 maximum_bitcast_fusion
  66.2 0.9 copy-done.1
  72.4 0.2 copy.158
  72.6 0.3 reduce_sum.24
  73.1 0.3 reshape.470
  73.5 0.2 fusion.63
  73.7 0.3 fusion.62
  74.8 0.2 convolution_add_fusion.13
  75.0 0.2 convolution_add_fusion.12
  75.4 0.2 convolution_add_fusion.10
  75.6 0.2 convolution_add_fusion.9
  75.7 0.2 convolution_add_fusion.8
  76.1 0.2 convolution_add_fusion.6
  76.3 0.2 convolution_add_fusion.5
  76.5 0.2 convolution_add_fusion.4
  76.8 0.2 convolution_add_fusion.2
  77.0 0.2 convolution_add_fusion.1
  77.2 0.2 fusion.4
  77.4 0.2 fusion.18
  77.7 0.2 fusion.16
  77.9 0.2 fusion.15
  78.1 0.2 fusion.14
  78.5 0.2 fusion.12
  78.7 0.2 fusion.11
  79.4 0.2 fusion.7
  79.9 0.6 copy.122
  80.5 0.8 reshape_reshape_reshape.3
  81.3 0.3 reduce_sum.22
  81.6 1.0 pad_maximum_fusion
  82.6 17.9 %all-to-all-start = ((f32[1,80,256]{1,0,2:T(1,128)}), f32[1,80,256]{1,0,2:T(1,128)S(1)}, u32[]{:S(2)}, u32[]{:S(2)}) async-start(f32[1,80,256]{1,0,2:T(1,128)} %pad_maximum_fusion), calls=%async_computation | async-start | bytes 262144 | tf_op jit(solution)/shard_map/all_to_all | solution.py:95
  100.5 0.3 fusion.49
  100.8 0.8 reshape.655
  101.6 9.5 %all-to-all-done = f32[1,80,256]{1,0,2:T(1,128)S(1)} async-done(((f32[1,80,256]{1,0,2:T(1,128)}), f32[1,80,256]{1,0,2:T(1,128)S(1)}, u32[]{:S(2)}, u32[]{:S(2)}) %all-to-all-start) | async-done | bytes 81952 | tf_op jit(solution)/shard_map/all_to_all | solution.py:95
  111.1 0.4 copy.197
  111.5 27.6 %gather_fusion.1 = f32[4096]{0:T(1024)S(1)} fusion(f32[2560,8]{1,0:T(8,128)S(1)} %bitcast.875, s32[4096]{0:T(1024)S(1)} %reshape.649), kind=kCustom, calls=%fused_computation.1.clone | custom fusion | bytes 65536 | tf_op jit(solution)/shard_map/jit(take_along_axis)/gather | solution.py:75
  139.1 0.9 reshape.652
  140.0 27.6 %gather_fusion = f32[4096]{0:T(1024)S(1)} fusion(f32[2560,8]{1,0:T(8,128)S(1)} %bitcast.876, s32[4096]{0:T(1024)S(1)} %reshape.643), kind=kCustom, calls=%fused_computation.clone | custom fusion | bytes 65536 | tf_op jit(solution)/shard_map/jit(take_along_axis)/gather | solution.py:75
  167.9 27.6 %gather_fusion.2 = f32[4096]{0:T(1024)S(1)} fusion(f32[2560,8]{1,0:T(8,128)S(1)} %bitcast.877, s32[4096]{0:T(1024)S(1)} %copy-done), kind=kCustom, calls=%fused_computation.2.clone | custom fusion | bytes 65536 | tf_op jit(solution)/shard_map/jit(take_along_axis)/gather | solution.py:75
  195.7 0.9 fusion.51
  196.6 0.7 copy.163
  (124 shorter events, 9.3 us)
Async XLA Ops:
  0.8 72.2 %collective-permute-start = (bf16[1,2,5,1024]{3,1,2,0:T(2,128)(2,1)S(1)}, bf16[1,2,5,1024]{3,1,2,0:T(2,128)(2,1)S(1)}, u32[]{:S(2)}, u32[]{:S(2)}) collective-permute-start(bf16[1,2,5,1024]{3,1,2,0:T(2,128)(2,1)S(1)} %get-tuple-element.72), channel_id=1, source_target_pairs={{0,1},{1,2},{2,3},{3,4},{4,5},{5,6},{6,7},{7,8},{8,9},{9,10},{10,1... | collective-permute-start | bytes 61448 | tf_op jit(solution)/shard_map/ppermute | solution.py:17
  4.2 68.8 %collective-permute-start.1 = (bf16[1,2,5,1024]{3,1,2,0:T(2,128)(2,1)S(1)}, bf16[1,2,5,1024]{3,1,2,0:T(2,128)(2,1)S(1)}, u32[]{:S(2)}, u32[]{:S(2)}) collective-permute-start(bf16[1,2,5,1024]{3,1,2,0:T(2,128)(2,1)S(1)} %get-tuple-element.73), channel_id=1, source_target_pairs={{1,0},{2,1},{3,2},{4,3},{5,4},{6,5},{7,6},{8,7},{9,8},{10,9},{11,1... | collective-permute-start | bytes 61448 | tf_op jit(solution)/shard_map/ppermute | solution.py:19
  6.8 58.2 %collective-permute-start.2 = (bf16[1,5,1024]{2,1,0:T(8,128)(2,1)}, bf16[1,5,1024]{2,1,0:T(8,128)(2,1)}, u32[]{:S(2)}, u32[]{:S(2)}) collective-permute-start(bf16[1,5,1024]{2,1,0:T(8,128)(2,1)} %get-tuple-element.74), channel_id=1, source_target_pairs={{0,1},{1,2},{2,3},{3,4},{4,5},{5,6},{6,7},{7,8},{8,9},{9,10},{10,1... | collective-permute-start | bytes 30728 | tf_op jit(solution)/shard_map/ppermute | solution.py:17
  12.0 53.0 %collective-permute-start.3 = (bf16[1,5,1024]{2,1,0:T(8,128)(2,1)S(1)}, bf16[1,5,1024]{2,1,0:T(8,128)(2,1)}, u32[]{:S(2)}, u32[]{:S(2)}) collective-permute-start(bf16[1,5,1024]{2,1,0:T(8,128)(2,1)S(1)} %get-tuple-element.75), channel_id=1, source_target_pairs={{1,0},{2,1},{3,2},{4,3},{5,4},{6,5},{7,6},{8,7},{9,8},{10,9},{11,1... | collective-permute-start | bytes 30728 | tf_op jit(solution)/shard_map/ppermute | solution.py:19
  21.2 1.3 copy-start.25
  21.2 1.4 copy-start.26
  21.2 1.4 copy-start.27
  21.2 3.4 %copy-start.17 = (bf16[2,11,256]{2,0,1:T(2,128)(2,1)S(1)}, bf16[2,11,256]{2,0,1:T(2,128)(2,1)}, u32[]{:S(2)}) copy-start(bf16[2,11,256]{2,0,1:T(2,128)(2,1)} %param.12) | copy-start | bytes 33796
  22.6 1.4 copy-start.5
  22.6 77.9 %copy-start.7 = (s32[1,1,512]{2,1,0:T(1,128)}, s32[1,1,512]{2,1,0:T(1,128)S(1)}, u32[]{:S(2)}) copy-start(s32[1,1,512]{2,1,0:T(1,128)S(1)} %fusion.61) | copy-start | bytes 6148
  22.6 1.3 copy-start.9
  22.7 1.3 copy-start.11
  22.7 1.3 copy-start.18
  22.7 1.3 copy-start.20
  22.7 1.3 copy-start.15
  22.7 77.8 %copy-start.13 = (s32[512]{0:T(512)}, s32[512]{0:T(512)S(1)}, u32[]{:S(2)}) copy-start(s32[512]{0:T(512)S(1)} %get-tuple-element.78) | copy-start | bytes 6148
  60.0 5.1 %copy-start.4 = (bf16[1,30,1024]{2,1,0:T(8,128)(2,1)S(1)}, bf16[1,30,1024]{2,1,0:T(8,128)(2,1)}, u32[]{:S(2)}) copy-start(bf16[1,30,1024]{2,1,0:T(8,128)(2,1)} %param.11) | copy-start | bytes 184324
  65.9 1.2 copy-start.1
  71.1 1.9 copy-start.3
  79.9 20.6 %copy-start.22 = (pred[512]{0:T(512)(128)(4,1)S(1)}, pred[512]{0:T(512)(128)(4,1)}, u32[]{:S(2)}) copy-start(pred[512]{0:T(512)(128)(4,1)} %get-tuple-element.77) | copy-start | bytes 1540
  82.6 28.5 %all-to-all-start = ((f32[1,80,256]{1,0,2:T(1,128)}), f32[1,80,256]{1,0,2:T(1,128)S(1)}, u32[]{:S(2)}, u32[]{:S(2)}) async-start(f32[1,80,256]{1,0,2:T(1,128)} %pad_maximum_fusion), calls=%async_computation | async-start | bytes 262144 | tf_op jit(solution)/shard_map/all_to_all | solution.py:95
  140.0 27.8 %copy-start = (s32[4096]{0:T(1024)S(1)}, s32[4096]{0:T(1024)}, u32[]{:S(2)}) copy-start(s32[4096]{0:T(1024)} %reshape.655) | copy-start | bytes 49156
  167.7 27.9 %copy-start.2 = (f32[1,512,8]{2,1,0:T(8,128)S(1)}, f32[1,512,8]{2,1,0:T(8,128)}, u32[]{:S(2)}) copy-start(f32[1,512,8]{2,1,0:T(8,128)} %reshape.652) | copy-start | bytes 49156
  167.8 27.9 %copy-start.6 = (s32[1,1,512]{2,1,0:T(1,128)S(1)}, s32[1,1,512]{2,1,0:T(1,128)}, u32[]{:S(2)}) copy-start(s32[1,1,512]{2,1,0:T(1,128)} %copy-done.5) | copy-start | bytes 6148
  167.8 27.9 %copy-start.8 = (s32[1,1,512]{2,1,0:T(1,128)S(1)}, s32[1,1,512]{2,1,0:T(1,128)}, u32[]{:S(2)}) copy-start(s32[1,1,512]{2,1,0:T(1,128)} %copy-done.7) | copy-start | bytes 6148
  167.8 27.9 %copy-start.10 = (s32[1,1,512]{2,1,0:T(1,128)S(1)}, s32[1,1,512]{2,1,0:T(1,128)}, u32[]{:S(2)}) copy-start(s32[1,1,512]{2,1,0:T(1,128)} %copy-done.9) | copy-start | bytes 6148
  167.8 27.9 %copy-start.12 = (s32[512]{0:T(512)S(1)}, s32[512]{0:T(512)}, u32[]{:S(2)}) copy-start(s32[512]{0:T(512)} %copy-done.11) | copy-start | bytes 6148
  167.8 27.9 %copy-start.14 = (s32[512]{0:T(512)S(1)}, s32[512]{0:T(512)}, u32[]{:S(2)}) copy-start(s32[512]{0:T(512)} %copy-done.13) | copy-start | bytes 6148
  167.8 27.9 %copy-start.16 = (s32[512]{0:T(512)S(1)}, s32[512]{0:T(512)}, u32[]{:S(2)}) copy-start(s32[512]{0:T(512)} %copy-done.15) | copy-start | bytes 6148
  167.8 27.9 %copy-start.19 = (pred[512]{0:T(512)(128)(4,1)S(1)}, pred[512]{0:T(512)(128)(4,1)}, u32[]{:S(2)}) copy-start(pred[512]{0:T(512)(128)(4,1)} %copy-done.18) | copy-start | bytes 1540
  167.8 27.9 %copy-start.21 = (pred[512]{0:T(512)(128)(4,1)S(1)}, pred[512]{0:T(512)(128)(4,1)}, u32[]{:S(2)}) copy-start(pred[512]{0:T(512)(128)(4,1)} %copy-done.20) | copy-start | bytes 1540
  167.8 27.9 %copy-start.23 = (pred[512]{0:T(512)(128)(4,1)S(1)}, pred[512]{0:T(512)(128)(4,1)}, u32[]{:S(2)}) copy-start(pred[512]{0:T(512)(128)(4,1)} %get-tuple-element.77) | copy-start | bytes 1540
  167.8 27.9 %copy-start.24 = (pred[512]{0:T(512)(128)(4,1)S(1)}, pred[512]{0:T(512)(128)(4,1)}, u32[]{:S(2)}) copy-start(pred[512]{0:T(512)(128)(4,1)} %get-tuple-element.76) | copy-start | bytes 1540
where the time goes:
time: 198 us; the launch traced here: 197 us
  local copies, waits for them, and re-layouts  141 us (71%)
  starting transfers between devices  29 us (15%)
  matrix products  11 us (6%)
  waiting for transfers between devices  9.53 us (5%)
  other arithmetic  4.92 us (2%)
    gather x9, local copies, waits for them, and re-layouts, lookup(): picked = jnp.take_along_axis(table, spread, axis=1)  85 us
    another operation x5, local copies, waits for them, and re-layouts, block_matrices(): tiled = jnp.tile(padded, [1] * (kernel.ndim - 1) + [block_len])  20.4 us
    all_to_all x1, starting transfers between devices, on_device(): lax.all_to_all(outgoing, 'wire', split_axis=2, concat_axis=1, tiled=True)  17.9 us
    dot_general x66, matrix products, deconvolve(): jnp.einsum('apwbr,pro->apwbo', source, matrices[:, offset, lag], preferre...  11 us
    all_to_all x1, waiting for transfers between devices, on_device(): lax.all_to_all(outgoing, 'wire', split_axis=2, concat_axis=1, tiled=True)  9.52 us
    ppermute x2, starting transfers between devices, extended(): lax.ppermute(tail, axis, [(i, (i + 1) % count) for i in range(ends)])  8.54 us
    reshape x2, local copies, waits for them, and re-layouts, block_matrices(): skewed = tiled.reshape(lead + (block_len, full_len - 1))  8.23 us
    slice x3, local copies, waits for them, and re-layouts, block_matrices(): kept = skewed[..., block_len:block_len + lag_count * block_len]  8.12 us
  transfers between devices with their start and end apart: 5, of which 1 were waited for; matrix products, arithmetic and copies ran while one was open for 30% of the time, Pallas kernels for 0%

commit v1 on v0

v1 whole, which is shorter than its diff:
```python
import jax
import jax.numpy as jnp
from jax import lax
from jax.experimental import pallas as pl
from jax.experimental.pallas import tpu as pltpu
from jax.sharding import PartitionSpec as P

LANES = 128
SUB = 8
REBIN = 4
GROUP = 32


def lane_iota(shape=(SUB, LANES)):
    return lax.broadcasted_iota(jnp.int32, shape, 1)


def between(lanes, low, high):
    return (lanes >= low) & (lanes < high)


def segments(widths, reach):
    starts, at = [], 0
    for width in widths:
        starts.append(at + reach)
        at += width + 2 * reach
    return starts


def conv_kernel(reach, indf, colf, indk, colk, out, kmat, toep, wide):
    taps = indk.shape[2]
    offsets = indk.shape[1]
    ticks = indf.shape[3]
    window = taps + LANES
    blocks = ticks // LANES
    bins = LANES // REBIN
    widths = (indf.shape[2], indf.shape[2], colf.shape[1])
    frames = (lambda: indf[0, 0], lambda: indf[0, 1], lambda: colf[0])

    kmat[...] = jnp.zeros_like(kmat)
    kmat[0:offsets, :] = indk[0]
    kmat[16:16 + offsets, :] = indk[1]
    kmat[32:32 + offsets, :] = colk[...]
    total = (lax.broadcasted_iota(jnp.int32, (taps, window), 0)
             + lax.broadcasted_iota(jnp.int32, (taps, window), 1))
    fold = between(total, taps, taps + REBIN).astype(jnp.float32).astype(jnp.bfloat16)
    rows = jnp.dot(kmat[...], fold, preferred_element_type=jnp.float32)

    lanes = lane_iota()
    subs = lax.broadcasted_iota(jnp.int32, (SUB, LANES), 0)
    pieces = window // LANES
    starts = segments(widths, reach)

    sums = []
    for plane in range(3):
        for offset in range(offsets):
            at = 16 * plane + offset
            flat = [jnp.broadcast_to(rows[at:at + 1, LANES * i:LANES * (i + 1)], (SUB, LANES))
                    for i in range(pieces)]
            made = []
            for part in range(bins // SUB):
                base = part * SUB * REBIN
                turned = [pltpu.roll(piece, base, 1, stride=REBIN, stride_axis=0) for piece in flat]
                keep = lanes >= base + REBIN * subs
                before = [jnp.zeros_like(turned[0])] + turned[:-1]
                made.append([jnp.where(keep, a, b) for a, b in zip(turned, before)])
            for pair in range(0, len(made), 2):
                at_row = offset * bins + pair * SUB
                for i in range(pieces):
                    exact = jnp.concatenate([made[pair][i], made[pair + 1][i]], axis=0)
                    high = exact.astype(jnp.bfloat16)
                    low = (exact - high.astype(jnp.float32)).astype(jnp.bfloat16)
                    toep[plane, at_row:at_row + 16, LANES * i:LANES * (i + 1)] = high
                    toep[plane, at_row:at_row + 16, window + LANES * i:window + LANES * (i + 1)] = low

        width = widths[plane]
        mine = frames[plane]()
        zeros = jnp.zeros((GROUP - width, ticks), jnp.bfloat16)
        padded = jnp.concatenate([mine, zeros], axis=0)
        blank = jnp.zeros((GROUP, LANES), jnp.bfloat16)
        history = taps // LANES
        tiles = [blank] * history + [padded[:, LANES * i:LANES * (i + 1)] for i in range(blocks)]
        for block in range(blocks):
            for i in range(pieces):
                piece = tiles[block + i]
                wide[plane, GROUP * block:GROUP * (block + 1), LANES * i:LANES * (i + 1)] = piece
                wide[plane, GROUP * block:GROUP * (block + 1), window + LANES * i:window + LANES * (i + 1)] = piece
        grid = lax.dot_general(
            toep[plane], wide[plane], (((1,), (1,)), ((), ())),
            preferred_element_type=jnp.float32)
        sums.append(grid)

    per_half = LANES // GROUP
    for half in range(blocks // per_half):
        for part in range(bins // SUB):
            gathered = []
            for plane in range(3):
                width = widths[plane]

                def moved(shift):
                    at_row = (reach - shift) * bins + part * SUB
                    piece = sums[plane][at_row:at_row + SUB, LANES * half:LANES * (half + 1)]
                    return piece if shift == 0 else pltpu.roll(piece, shift % LANES, 1)

                spare = GROUP - width
                runs, shift = [], 0
                while shift <= reach:
                    last = min(reach, shift + spare if shift > 0 else spare)
                    runs.append((shift, last))
                    shift = last + 1
                shift = 1
                while shift <= reach:
                    last = min(reach, shift + spare)
                    runs.append((-last, -shift))
                    shift = last + 1
                for first, last in runs:
                    acc = moved(first)
                    for step in range(first + 1, last + 1):
                        acc = acc + moved(step)
                    gathered.append((plane, first, last + width, acc))
            for spot in range(per_half):
                tile = (half * per_half + spot) * (bins // SUB) + part
                result = jnp.zeros((SUB, LANES), jnp.float32)
                for plane, first, end, acc in gathered:
                    start = starts[plane]
                    placed = pltpu.roll(acc, (start - GROUP * spot) % LANES, 1)
                    valid = between(lanes, start + first, start + end)
                    result = result + jnp.where(valid, placed, 0.0)
                out[tile] = result


def cell_kernel(reach, widths, counts, cell_u, cell_v, cell_w, table, out, joined):
    sources = table.shape[0]
    lanes = lane_iota()
    starts = segments(widths, reach)

    index = lanes
    target = lanes < 0
    from_next = lanes < 0
    for start, width in zip(starts, widths):
        early = between(lanes, start, start + reach)
        late = between(lanes, start + width - reach, start + width)
        index = jnp.where(early, lanes + width, index)
        index = jnp.where(late, lanes - width, index)
        target = target | early | late
        from_next = from_next | between(lanes, start - reach, start)
    zero = jnp.zeros((SUB, LANES), jnp.float32)
    for source in range(sources):
        after = table[source + 1] if source + 1 < sources else zero
        before = table[source - 1] if source > 0 else zero
        both = jnp.where(from_next, after, before)
        extra = jnp.take_along_axis(both, index, axis=1)
        joined[source] = table[source] + jnp.where(target, extra, 0.0)

    count = counts[0, 0]
    cells = cell_u.shape[2]
    for chunk in range(cells // LANES):
        span = slice(chunk * LANES, (chunk + 1) * LANES)
        charge = None
        for cell, start, width in zip((cell_u, cell_v, cell_w), starts, widths):
            wire = jnp.broadcast_to(cell[0, 0:1, span], (SUB, LANES))
            owner = (wire * ((1 << 18) // width + 1)) >> 18
            spot = wire - owner * width + start
            picked = zero
            for source in range(sources):
                value = jnp.take_along_axis(joined[source], spot, axis=1)
                picked = jnp.where(owner == source, value, picked)
            charge = picked if charge is None else jnp.minimum(charge, picked)
        live = lanes + chunk * LANES < count
        out[0, 0, :, span] = jnp.where(live, charge, 0.0)


def on_device(ind_frames, col_frames, ind_kernel, col_kernel, cell_u, cell_v, cell_w, tile_counts):
    reach = (ind_kernel.shape[1] - 1) // 2
    taps = ind_kernel.shape[2]
    offsets = ind_kernel.shape[1]
    ticks = ind_frames.shape[3]
    widths = (ind_frames.shape[2], ind_frames.shape[2], col_frames.shape[1])
    bins = LANES // REBIN
    tiles = ticks // REBIN // SUB
    window = taps + LANES
    blocks = ticks // LANES
    vmem = pl.BlockSpec(memory_space=pltpu.VMEM)
    outgoing = pl.pallas_call(
        lambda *refs: conv_kernel(reach, *refs),
        out_shape=jax.ShapeDtypeStruct((tiles, SUB, LANES), jnp.float32),
        in_specs=[vmem] * 4,
        out_specs=vmem,
        scratch_shapes=[
            pltpu.VMEM((48, taps), jnp.bfloat16),
            pltpu.VMEM((3, offsets * bins, 2 * window), jnp.bfloat16),
            pltpu.VMEM((3, GROUP * blocks, 2 * window), jnp.bfloat16),
        ],
        name="deconvolve",
    )(ind_frames, col_frames, ind_kernel, col_kernel)
    arrived = lax.all_to_all(outgoing, "wire", split_axis=0, concat_axis=0, tiled=True)
    return pl.pallas_call(
        lambda *refs: cell_kernel(reach, widths, *refs),
        out_shape=jax.ShapeDtypeStruct((1, 1, SUB, cell_u.shape[2]), jnp.float32),
        in_specs=[pl.BlockSpec(memory_space=pltpu.SMEM)] + [vmem] * 4,
        out_specs=vmem,
        scratch_shapes=[pltpu.VMEM((tiles, SUB, LANES), jnp.float32)],
        name="cells",
    )(tile_counts, cell_u, cell_v, cell_w, arrived)


def solution(mesh):
    return jax.shard_map(
        on_device,
        mesh=mesh,
        in_specs=(
            P("apa", None, "wire", None),
            P("apa", "wire", None),
            P(),
            P(),
            P("apa", "wire", None),
            P("apa", "wire", None),
            P("apa", "wire", None),
            P("apa", "wire"),
        ),
        out_specs=P("apa", "wire", None, None),
        check_vma=False,
    )
```

time: 198 us -> 32 us (0.16)
  local copies, waits for them, and re-layouts: 141 us -> 2.83 us
  starting transfers between devices: 29 us -> 13.2 us
  matrix products: 11 us -> 0 us
  Pallas kernels: 0 us -> 5.23 us
  other arithmetic: 4.92 us -> 0 us
    gather x9 -> x0, local copies, waits for them, and re-layouts: 85 us -> none  [lookup(): picked = jnp.take_along_axis(table, spread, axis=1)]
    another operation x6 -> x0, local copies, waits for them, and re-layouts: 21.1 us -> none  [the longest x5 20.4 us: block_matrices(): tiled = jnp.tile(padded, [1] * (kernel.ndim - 1) + [block_len])]
    slice x11 -> x0, local copies, waits for them, and re-layouts: 15.1 us -> none  [the longest x3 8.12 us: block_matrices(): kept = skewed[..., block_len:block_len + lag_count * block_len]]
    reshape x6 -> x0, local copies, waits for them, and re-layouts: 13.9 us -> none  [the longest x2 8.23 us: block_matrices(): skewed = tiled.reshape(lead + (block_len, full_len - 1))]
    ppermute x4 -> x0, starting transfers between devices: 11.1 us -> none  [the longest x2 8.54 us: extended(): lax.ppermute(tail, axis, [(i, (i + 1) % count) for i in range(ends)])]
    dot_general x66 -> x0, matrix products: 11 us -> none  [deconvolve(): jnp.einsum('apwbr,pro->apwbo', source, matrices[:, offset, lag], preferre...]
    pallas_call x0 -> x2, Pallas kernels: none -> 5.23 us  [the longest x1 3.08 us: on_device(): pl.pallas_call(lambda *refs: conv_kernel(reach, *refs), out_shape=jax.Sha...]
    all_to_all x1, starting transfers between devices: 17.9 us -> 13.2 us  [on_device(): lax.all_to_all(outgoing, 'wire', split_axis=0, concat_axis=0, tiled=True)]
  transfers between devices with their start and end apart: 5 -> 1, of which waited for: 1 -> 1; matrix products, arithmetic and copies ran while one was open for 30% -> 0% of each run, Pallas kernels for 0% -> 0%
where the time goes in v1:
time: 32 us; the launch traced here: 31.7 us
  starting transfers between devices  13.2 us (41%)
  waiting for transfers between devices  9.8 us (31%)
  Pallas kernels  5.23 us (16%)
  local copies, waits for them, and re-layouts  2.83 us (9%)
  between operations  0.66 us (2%)
    all_to_all x1, starting transfers between devices, on_device(): lax.all_to_all(outgoing, 'wire', split_axis=0, concat_axis=0, tiled=True)  13.2 us
    all_to_all x1, waiting for transfers between devices, on_device(): lax.all_to_all(outgoing, 'wire', split_axis=0, concat_axis=0, tiled=True)  9.8 us
    pallas_call x1, Pallas kernels, on_device(): pl.pallas_call(lambda *refs: conv_kernel(reach, *refs), out_shape=jax.Sha...  3.08 us
    unnamed x6, local copies, waits for them, and re-layouts  2.83 us
    pallas_call x1, Pallas kernels, on_device(): pl.pallas_call(lambda *refs: cell_kernel(reach, widths, *refs), out_shape...  2.15 us
  transfers between devices with their start and end apart: 1, of which 1 were waited for; matrix products, arithmetic and copies ran while one was open for 0% of the time, Pallas kernels for 0%

profile of v1, /device:TPU:56, one launch (start us, length us, event | category | flops | bytes accessed | tf_op | source)
XLA Modules:
  0.0 31.7 jit_solution(8280794717348252632)
XLA Ops:
  0.0 0.0 copy-start.1
  0.0 1.6 %copy.9.refs_0_ = bf16[1,2,25,1024]{3,2,1,0:T(8,128)(2,1)} copy(bf16[1,2,25,1024]{3,1,2,0:T(2,128)(2,1)} %param.8) | data formatting | bytes 204800 | tf_op args[0]
  1.6 0.0 copy-done.1
  1.6 0.6 %copy.10.refs_2_ = bf16[2,11,256]{2,1,0:T(8,128)(2,1)} copy(bf16[2,11,256]{2,0,1:T(2,128)(2,1)S(1)} %copy-done.1) | data formatting | bytes 22528 | tf_op args[2]
  2.2 3.1 %deconvolve.1 = f32[32,8,128]{2,1,0:T(8,128)} custom-call(bf16[1,2,25,1024]{3,2,1,0:T(8,128)(2,1)} %copy.9.refs_0_, bf16[1,30,1024]{2,1,0:T(8,128)(2,1)} %refs_1_.2, bf16[2,11,256]{2,1,0:T(8,128)(2,1)} %copy.10.refs_2_, bf16[11,256]{1,0:T(8,128)(2,1)} %refs_3_.2), custom_call_target="tpu_custom_call" | custom-call | tf_op jit(solution)/shard_map/deconvolve/pallas_call | solution.py:184
  5.3 13.2 %all-to-all-start = ((f32[32,8,128]{2,1,0:T(8,128)}), f32[32,8,128]{2,1,0:T(8,128)S(1)}, u32[]{:S(2)}, u32[]{:S(2)}) async-start(f32[32,8,128]{2,1,0:T(8,128)} %deconvolve.1), calls=%async_computation | async-start | bytes 262144 | tf_op jit(solution)/shard_map/all_to_all | solution.py:196
  19.1 9.8 %all-to-all-done.refs_4_ = f32[32,8,128]{2,1,0:T(8,128)S(1)} async-done(((f32[32,8,128]{2,1,0:T(8,128)}), f32[32,8,128]{2,1,0:T(8,128)S(1)}, u32[]{:S(2)}, u32[]{:S(2)}) %all-to-all-start) | async-done | bytes 131104 | tf_op jit(solution)/shard_map/all_to_all | solution.py:196
  28.9 0.0 copy-start
  28.9 0.6 %copy-done = f32[32,8,128]{2,1,0:T(8,128)} copy-done((f32[32,8,128]{2,1,0:T(8,128)}, f32[32,8,128]{2,1,0:T(8,128)S(1)}, u32[]{:S(2)}) %copy-start) | copy-done | bytes 131096
  29.5 2.1 %cells.1 = f32[1,1,8,512]{3,2,1,0:T(8,128)} custom-call(s32[1,1]{1,0:T(1,128)S(6)} %copy.11.refs_0_, s32[1,1,512]{2,1,0:T(1,128)} %refs_1_.3, s32[1,1,512]{2,1,0:T(1,128)} %refs_2_.2, s32[1,1,512]{2,1,0:T(1,128)} %refs_3_.3, f32[32,8,128]{2,1,0:T(8,128)} %copy-done), custom_call_target="tpu_custom_call" | custom-call | tf_op jit(solution)/shard_map/cells/pallas_call | solution.py:197
Async XLA Ops:
  0.0 1.6 %copy-start.1 = (bf16[2,11,256]{2,0,1:T(2,128)(2,1)S(1)}, bf16[2,11,256]{2,0,1:T(2,128)(2,1)}, u32[]{:S(2)}) copy-start(bf16[2,11,256]{2,0,1:T(2,128)(2,1)} %param.10) | copy-start | bytes 33796
  5.3 23.6 %all-to-all-start = ((f32[32,8,128]{2,1,0:T(8,128)}), f32[32,8,128]{2,1,0:T(8,128)S(1)}, u32[]{:S(2)}, u32[]{:S(2)}) async-start(f32[32,8,128]{2,1,0:T(8,128)} %deconvolve.1), calls=%async_computation | async-start | bytes 262144 | tf_op jit(solution)/shard_map/all_to_all | solution.py:196
  28.9 0.6 %copy-start = (f32[32,8,128]{2,1,0:T(8,128)}, f32[32,8,128]{2,1,0:T(8,128)S(1)}, u32[]{:S(2)}) copy-start(f32[32,8,128]{2,1,0:T(8,128)S(1)} %all-to-all-done.refs_4_) | copy-start | bytes 393220

commit v2 on v1

--- a/solution.py
+++ b/solution.py
@@ -27,24 +27,28 @@
     return starts
 
 
-def conv_kernel(reach, indf, colf, indk, colk, out, kmat, toep, wide):
-    taps = indk.shape[2]
-    offsets = indk.shape[1]
-    ticks = indf.shape[3]
+def conv_kernel(reach, widths, ind_hbm, col_hbm, indk_hbm, colk_hbm, out, indf, colf, indk, colk, sems, toep, wide):
+    copies = [pltpu.make_async_copy(source, target, sems.at[i]) for i, (source, target) in enumerate(
+        ((indk_hbm, indk), (colk_hbm, colk), (ind_hbm, indf), (col_hbm, colf)))]
+    for copy in copies:
+        copy.start()
+    offsets, taps = colk.shape
+    ticks = colf.shape[2]
     window = taps + LANES
     blocks = ticks // LANES
+    history = taps // LANES
     bins = LANES // REBIN
-    widths = (indf.shape[2], indf.shape[2], colf.shape[1])
-    frames = (lambda: indf[0, 0], lambda: indf[0, 1], lambda: colf[0])
-
-    kmat[...] = jnp.zeros_like(kmat)
-    kmat[0:offsets, :] = indk[0]
-    kmat[16:16 + offsets, :] = indk[1]
-    kmat[32:32 + offsets, :] = colk[...]
-    total = (lax.broadcasted_iota(jnp.int32, (taps, window), 0)
-             + lax.broadcasted_iota(jnp.int32, (taps, window), 1))
-    fold = between(total, taps, taps + REBIN).astype(jnp.float32).astype(jnp.bfloat16)
-    rows = jnp.dot(kmat[...], fold, preferred_element_type=jnp.float32)
+
+    total = (lax.broadcasted_iota(jnp.int32, (LANES, window), 0)
+             + lax.broadcasted_iota(jnp.int32, (LANES, window), 1))
+    fold = [between(total + LANES * i, taps, taps + REBIN).astype(jnp.float32).astype(jnp.bfloat16)
+            for i in range(history)]
+    fold = jnp.concatenate(fold, axis=0)
+    copies[0].wait()
+    copies[1].wait()
+    both = indk[...]
+    rows_of = [jnp.dot(k, fold, preferred_element_type=jnp.float32)
+               for k in (both[:, 0, :], both[:, 1, :], colk[...])]
 
     lanes = lane_iota()
     subs = lax.broadcasted_iota(jnp.int32, (SUB, LANES), 0)
@@ -54,7 +58,7 @@
     sums = []
     for plane in range(3):
         for offset in range(offsets):
-            at = 16 * plane + offset
+            rows, at = rows_of[plane], offset
             flat = [jnp.broadcast_to(rows[at:at + 1, LANES * i:LANES * (i + 1)], (SUB, LANES))
                     for i in range(pieces)]
             made = []
@@ -73,13 +77,25 @@
                     toep[plane, at_row:at_row + 16, LANES * i:LANES * (i + 1)] = high
                     toep[plane, at_row:at_row + 16, window + LANES * i:window + LANES * (i + 1)] = low
 
+    copies[2].wait()
+    copies[3].wait()
+    height = GROUP * blocks
+    place = lax.broadcasted_iota(jnp.int32, (height, indf.shape[0]), 0)
+    source = lax.broadcasted_iota(jnp.int32, (height, indf.shape[0]), 1)
+    wanted = ((place & (GROUP - 1)) * blocks + place // GROUP) * 2
+    ordered = [jnp.dot((source == wanted + p).astype(jnp.float32).astype(jnp.bfloat16), indf[...],
+                       preferred_element_type=jnp.float32).astype(jnp.bfloat16) for p in range(2)]
+
+    for plane in range(3):
         width = widths[plane]
-        mine = frames[plane]()
-        zeros = jnp.zeros((GROUP - width, ticks), jnp.bfloat16)
-        padded = jnp.concatenate([mine, zeros], axis=0)
         blank = jnp.zeros((GROUP, LANES), jnp.bfloat16)
-        history = taps // LANES
-        tiles = [blank] * history + [padded[:, LANES * i:LANES * (i + 1)] for i in range(blocks)]
+        if plane < 2:
+            tiles = [ordered[plane][GROUP * i:GROUP * (i + 1)] for i in range(blocks)]
+        else:
+            spare = jnp.zeros((GROUP - width, ticks), jnp.bfloat16)
+            padded = jnp.concatenate([colf[0], spare], axis=0)
+            tiles = [padded[:, LANES * i:LANES * (i + 1)] for i in range(blocks)]
+        tiles = [blank] * history + tiles
         for block in range(blocks):
             for i in range(pieces):
                 piece = tiles[block + i]
@@ -181,18 +197,24 @@
     window = taps + LANES
     blocks = ticks // LANES
     vmem = pl.BlockSpec(memory_space=pltpu.VMEM)
+    ind_rows = ind_frames.reshape(2, widths[0], blocks, LANES).transpose(1, 2, 0, 3).reshape(-1, LANES)
+    ind_taps = ind_kernel.transpose(1, 0, 2)
     outgoing = pl.pallas_call(
-        lambda *refs: conv_kernel(reach, *refs),
+        lambda *refs: conv_kernel(reach, widths, *refs),
         out_shape=jax.ShapeDtypeStruct((tiles, SUB, LANES), jnp.float32),
-        in_specs=[vmem] * 4,
+        in_specs=[pl.BlockSpec(memory_space=pl.ANY)] * 4,
         out_specs=vmem,
         scratch_shapes=[
-            pltpu.VMEM((48, taps), jnp.bfloat16),
+            pltpu.VMEM(ind_rows.shape, jnp.bfloat16),
+            pltpu.VMEM(col_frames.shape, jnp.bfloat16),
+            pltpu.VMEM(ind_taps.shape, jnp.bfloat16),
+            pltpu.VMEM(col_kernel.shape, jnp.bfloat16),
+            pltpu.SemaphoreType.DMA((4,)),
             pltpu.VMEM((3, offsets * bins, 2 * window), jnp.bfloat16),
             pltpu.VMEM((3, GROUP * blocks, 2 * window), jnp.bfloat16),
         ],
         name="deconvolve",
-    )(ind_frames, col_frames, ind_kernel, col_kernel)
+    )(ind_rows, col_frames, ind_taps, col_kernel)
     arrived = lax.all_to_all(outgoing, "wire", split_axis=0, concat_axis=0, tiled=True)
     return pl.pallas_call(
         lambda *refs: cell_kernel(reach, widths, *refs),
@@ -201,6 +223,7 @@
         out_specs=vmem,
         scratch_shapes=[pltpu.VMEM((tiles, SUB, LANES), jnp.float32)],
         name="cells",
+        compiler_params=pltpu.CompilerParams(vmem_limit_bytes=4 << 20),
     )(tile_counts, cell_u, cell_v, cell_w, arrived)
 
 

time: 32 us -> 28.5 us (0.89)
  local copies, waits for them, and re-layouts: 2.83 us -> 0.02 us
  Pallas kernels: 5.23 us -> 4.45 us
    unnamed x6, local copies, waits for them, and re-layouts: 2.83 us -> 0.02 us
    pallas_call x1, Pallas kernels: 2.15 us -> 1.2 us  [on_device(): pl.pallas_call(lambda *refs: cell_kernel(reach, widths, *refs), out_shape...]
where the time goes in v2:
time: 28.5 us; the launch traced here: 28.3 us
  starting transfers between devices  13.3 us (47%)
  waiting for transfers between devices  9.8 us (34%)
  Pallas kernels  4.45 us (16%)
  between operations  0.69 us (2%)
    all_to_all x1, starting transfers between devices, on_device(): lax.all_to_all(outgoing, 'wire', split_axis=0, concat_axis=0, tiled=True)  13.3 us
    all_to_all x1, waiting for transfers between devices, on_device(): lax.all_to_all(outgoing, 'wire', split_axis=0, concat_axis=0, tiled=True)  9.8 us
    pallas_call x1, Pallas kernels, on_device(): pl.pallas_call(lambda *refs: conv_kernel(reach, widths, *refs), out_shape...  3.26 us
    pallas_call x1, Pallas kernels, on_device(): pl.pallas_call(lambda *refs: cell_kernel(reach, widths, *refs), out_shape...  1.2 us
  transfers between devices with their start and end apart: 1, of which 1 were waited for; matrix products, arithmetic and copies ran while one was open for 0% of the time, Pallas kernels for 0%

profile of v2, /device:TPU:56, one launch (start us, length us, event | category | flops | bytes accessed | tf_op | source)
XLA Modules:
  0.0 28.3 jit_solution(14173701956564144292)
XLA Ops:
  0.0 3.3 %deconvolve.1 = f32[32,8,128]{2,1,0:T(8,128)} custom-call(bf16[400,128]{1,0:T(8,128)(2,1)} %bitcast.6, bf16[1,30,1024]{2,1,0:T(8,128)(2,1)} %refs_1_.2, bf16[11,2,256]{2,1,0:T(2,128)(2,1)} %bitcast.7, bf16[11,256]{1,0:T(8,128)(2,1)} %refs_3_.2), custom_call_target="tpu_custom_call" | custom-call | tf_op jit(solution)/shard_map/deconvolve/pallas_call | solution.py:202
  3.3 0.0 copy-start
  3.3 0.0 copy-start.1
  3.3 0.0 copy-start.2
  3.3 13.3 %all-to-all-start = ((f32[32,8,128]{2,1,0:T(8,128)}), f32[32,8,128]{2,1,0:T(8,128)S(1)}, u32[]{:S(2)}, u32[]{:S(2)}) async-start(f32[32,8,128]{2,1,0:T(8,128)} %deconvolve.1), calls=%async_computation | async-start | bytes 262144 | tf_op jit(solution)/shard_map/all_to_all | solution.py:218
  17.3 9.8 %all-to-all-done.refs_4_ = f32[32,8,128]{2,1,0:T(8,128)S(1)} async-done(((f32[32,8,128]{2,1,0:T(8,128)}), f32[32,8,128]{2,1,0:T(8,128)S(1)}, u32[]{:S(2)}, u32[]{:S(2)}) %all-to-all-start) | async-done | bytes 131104 | tf_op jit(solution)/shard_map/all_to_all | solution.py:218
  27.1 0.0 copy-done
  27.1 0.0 copy-done.1
  27.1 0.0 copy-done.2
  27.1 1.2 %cells.1 = f32[1,1,8,512]{3,2,1,0:T(8,128)} custom-call(s32[1,1]{1,0:T(1,128)S(6)} %copy.10.refs_0_, s32[1,1,512]{2,1,0:T(1,128)S(1)} %copy-done, s32[1,1,512]{2,1,0:T(1,128)S(1)} %copy-done.1, s32[1,1,512]{2,1,0:T(1,128)S(1)} %copy-done.2, f32[32,8,128]{2,1,0:T(8,128)S(1)} %all-to-all-done.refs_4_), custom_call_target="tpu_custom_call" | custom-call | tf_op jit(solution)/shard_map/cells/pallas_call | solution.py:219
Async XLA Ops:
  3.3 23.8 %copy-start = (s32[1,1,512]{2,1,0:T(1,128)S(1)}, s32[1,1,512]{2,1,0:T(1,128)}, u32[]{:S(2)}) copy-start(s32[1,1,512]{2,1,0:T(1,128)} %refs_1_.3) | copy-start | bytes 6148
  3.3 23.8 %copy-start.1 = (s32[1,1,512]{2,1,0:T(1,128)S(1)}, s32[1,1,512]{2,1,0:T(1,128)}, u32[]{:S(2)}) copy-start(s32[1,1,512]{2,1,0:T(1,128)} %refs_2_.1) | copy-start | bytes 6148
  3.3 23.8 %copy-start.2 = (s32[1,1,512]{2,1,0:T(1,128)S(1)}, s32[1,1,512]{2,1,0:T(1,128)}, u32[]{:S(2)}) copy-start(s32[1,1,512]{2,1,0:T(1,128)} %refs_3_.3) | copy-start | bytes 6148
  3.3 23.8 %all-to-all-start = ((f32[32,8,128]{2,1,0:T(8,128)}), f32[32,8,128]{2,1,0:T(8,128)S(1)}, u32[]{:S(2)}, u32[]{:S(2)}) async-start(f32[32,8,128]{2,1,0:T(8,128)} %deconvolve.1), calls=%async_computation | async-start | bytes 262144 | tf_op jit(solution)/shard_map/all_to_all | solution.py:218

commit v3 on v2

v3 whole, which is shorter than its diff:
```python
import jax
import jax.numpy as jnp
from jax import lax
from jax.experimental import pallas as pl
from jax.experimental.pallas import tpu as pltpu
from jax.sharding import PartitionSpec as P

LANES = 128
SUB = 8
REBIN = 4
GROUP = 32
TURN = LANES // GROUP
RIGHT = 0
LEFT = 16


def lane_iota():
    return lax.broadcasted_iota(jnp.int32, (SUB, LANES), 1)


def between(lanes, low, high):
    return (lanes >= low) & (lanes < high)


def conv_kernel(reach, widths, ind_hbm, col_hbm, indk_hbm, colk_hbm, u_hbm, v_hbm, w_hbm, count_hbm,
                out, where_out, indf, colf, indk, colk, cells, count, sems, toep, wide):
    copies = [pltpu.make_async_copy(source, target, sems.at[i]) for i, (source, target) in enumerate((
        (indk_hbm, indk), (colk_hbm, colk), (ind_hbm, indf), (col_hbm, colf),
        (u_hbm, cells.at[0]), (v_hbm, cells.at[1]), (w_hbm, cells.at[2]), (count_hbm, count)))]
    for copy in copies:
        copy.start()
    offsets, taps = colk.shape
    ticks = colf.shape[2]
    window = taps + LANES
    blocks = ticks // LANES
    history = taps // LANES
    bins = LANES // REBIN
    pieces = window // LANES
    lanes = lane_iota()
    subs = lax.broadcasted_iota(jnp.int32, (SUB, LANES), 0)

    total = (lax.broadcasted_iota(jnp.int32, (taps, window), 0)
             + lax.broadcasted_iota(jnp.int32, (taps, window), 1))
    fold = between(total, taps, taps + REBIN).astype(jnp.float32).astype(jnp.bfloat16)
    height = GROUP * blocks
    place = lax.broadcasted_iota(jnp.int32, (height, indf.shape[0]), 0)
    source = lax.broadcasted_iota(jnp.int32, (height, indf.shape[0]), 1)
    wanted = ((place & (GROUP - 1)) * blocks + place // GROUP) * 2
    pick = [(source == wanted + p).astype(jnp.float32).astype(jnp.bfloat16) for p in range(2)]

    for copy in copies:
        copy.wait()

    both = indk[...]
    rows_of = [jnp.dot(k, fold, preferred_element_type=jnp.float32)
               for k in (both[:, 0, :], both[:, 1, :], colk[...])]

    sums = []
    for plane in range(3):
        width = widths[plane]
        blank = jnp.zeros((GROUP, LANES), jnp.bfloat16)
        if plane < 2:
            ordered = jnp.dot(pick[plane], indf[...], preferred_element_type=jnp.float32).astype(jnp.bfloat16)
            tiles = [ordered[GROUP * i:GROUP * (i + 1)] for i in range(blocks)]
        else:
            spare = jnp.zeros((GROUP - width, ticks), jnp.bfloat16)
            padded = jnp.concatenate([colf[0], spare], axis=0)
            tiles = [padded[:, LANES * i:LANES * (i + 1)] for i in range(blocks)]
        tiles = [blank] * history + tiles
        for block in range(blocks):
            for i in range(pieces):
                piece = tiles[block + i]
                wide[plane, GROUP * block:GROUP * (block + 1), LANES * i:LANES * (i + 1)] = piece
                wide[plane, GROUP * block:GROUP * (block + 1), window + LANES * i:window + LANES * (i + 1)] = piece
        for offset in range(offsets):
            row = rows_of[plane][offset:offset + 1, :]
            flat = [jnp.broadcast_to(row[:, LANES * i:LANES * (i + 1)], (SUB, LANES)) for i in range(pieces)]
            made = []
            for part in range(bins // SUB):
                base = part * SUB * REBIN
                turned = [pltpu.roll(piece, base, 1, stride=REBIN, stride_axis=0) for piece in flat]
                keep = lanes >= base + REBIN * subs
                before = [jnp.zeros_like(turned[0])] + turned[:-1]
                made.append([jnp.where(keep, a, b) for a, b in zip(turned, before)])
            for pair in range(0, len(made), 2):
                at_row = offset * bins + pair * SUB
                for i in range(pieces):
                    exact = jnp.concatenate([made[pair][i], made[pair + 1][i]], axis=0)
                    high = exact.astype(jnp.bfloat16)
                    low = (exact - high.astype(jnp.float32)).astype(jnp.bfloat16)
                    toep[plane, at_row:at_row + 16, LANES * i:LANES * (i + 1)] = high
                    toep[plane, at_row:at_row + 16, window + LANES * i:window + LANES * (i + 1)] = low
        grid = lax.dot_general(
            toep[plane], wide[plane], (((1,), (1,)), ((), ())),
            preferred_element_type=jnp.float32)
        sums.append(grid)

    for plane in range(3):
        width = widths[plane]
        for chunk in range(cells.shape[3] // LANES):
            span = slice(chunk * LANES, (chunk + 1) * LANES)
            wire = jnp.broadcast_to(cells[plane, 0, 0:1, span], (SUB, LANES))
            owner = (wire * ((1 << 18) // width + 1)) >> 18
            spot = wire - owner * width + ((owner + plane) & (TURN - 1)) * GROUP
            spot = spot + (owner // TURN) * LANES
            live = lanes + chunk * LANES < count[0, 0]
            where_out[plane, :, span] = jnp.where(live, spot, -1)

    turn = (lax.axis_index("wire") & (TURN - 1)) * GROUP
    spots = (lanes - turn) & (LANES - 1)
    slot = lanes & (GROUP - 1)
    per_half = LANES // GROUP
    for half in range(blocks // per_half):
        for part in range(bins // SUB):
            gathered = []
            for plane in range(3):
                width = widths[plane]
                spare = GROUP - width

                def run(first, last):
                    acc = None
                    for shift in range(first, last + 1):
                        at_row = (reach - shift) * bins + part * SUB
                        piece = sums[plane][at_row:at_row + SUB, LANES * half:LANES * (half + 1)]
                        piece = piece if shift == 0 else pltpu.roll(piece, shift % LANES, 1)
                        acc = piece if acc is None else acc + piece
                    return acc

                if spare >= reach:
                    after, before = run(0, reach), run(-reach, -1)
                    main = after + before
                else:
                    near, far = run(0, spare), run(spare + 1, reach)
                    main = near + jnp.where(slot > spare, far, 0.0)
                    after = jnp.where(slot >= width, near, 0.0) + far
                    near, far = run(-spare, -1), run(-reach, -spare - 1)
                    main = main + near + jnp.where(slot < GROUP - reach, far, 0.0)
                    before = jnp.where(slot >= width, near, 0.0) + far
                extra = (TURN - 1) * GROUP + reach * plane
                gathered += [(main, 0, GROUP * plane, width),
                             (after, width, extra + RIGHT, reach),
                             (before, -reach, extra + LEFT, reach)]
            for spot in range(per_half):
                tile = (half * per_half + spot) * (bins // SUB) + part
                result = jnp.zeros((SUB, LANES), jnp.float32)
                for acc, begin, target, size in gathered:
                    amount = (turn + (target - begin - GROUP * spot) % LANES) & (LANES - 1)
                    placed = pltpu.roll(acc, amount, 1)
                    result = jnp.where(between(spots, target, target + size), placed, result)
                out[tile] = result


def cell_kernel(reach, widths, table, wanted, out):
    sources = table.shape[0]
    lanes = lane_iota()
    group = lanes // GROUP
    slot = lanes & (GROUP - 1)
    zero = jnp.zeros((SUB, LANES), jnp.float32)

    def joined(stage, plane):
        made = None
        for i in range(TURN):
            piece = table[stage * TURN + i]
            made = piece if made is None else jnp.where(group == (plane + i) % TURN, piece, made)
        return made

    stages = sources // TURN
    halos = [joined(stage, TURN - 1) for stage in range(stages)]
    early = (group == TURN - 2) & (slot < LEFT)
    late = (group == TURN - 1) & (slot >= LEFT)
    mixed = []
    for stage in range(stages):
        made = jnp.where(early, halos[stage - 1] if stage > 0 else zero, halos[stage])
        mixed.append(jnp.where(late, halos[stage + 1] if stage + 1 < stages else zero, made))
    full = []
    for plane in range(3):
        width = widths[plane]
        first = slot < reach
        last = between(slot, width - reach, width)
        index = jnp.where(
            first, ((group - plane + 2) & (TURN - 1)) * GROUP + RIGHT + reach * plane + slot,
            ((group - plane) & (TURN - 1)) * GROUP + LEFT + reach * plane + slot - (width - reach))
        index = jnp.where(first | last, index, lanes)
        full.append([joined(stage, plane) + jnp.where(
            first | last, jnp.take_along_axis(mixed[stage], index, axis=1), 0.0) for stage in range(stages)])

    for chunk in range(wanted.shape[2] // LANES):
        span = slice(chunk * LANES, (chunk + 1) * LANES)
        charge = None
        for plane in range(3):
            at = wanted[plane, :, span]
            stage_of, lane_of = at >> 7, at & (LANES - 1)
            picked = zero
            for stage in range(stages):
                value = jnp.take_along_axis(full[plane][stage], lane_of, axis=1)
                picked = jnp.where(stage_of == stage, value, picked)
            charge = picked if charge is None else jnp.minimum(charge, picked)
        out[0, 0, :, span] = charge


def on_device(ind_frames, col_frames, ind_kernel, col_kernel, cell_u, cell_v, cell_w, tile_counts):
    offsets, taps = col_kernel.shape
    reach = (offsets - 1) // 2
    ticks = ind_frames.shape[3]
    widths = (ind_frames.shape[2], ind_frames.shape[2], col_frames.shape[1])
    bins = LANES // REBIN
    tiles = ticks // REBIN // SUB
    window = taps + LANES
    blocks = ticks // LANES
    ind_rows = ind_frames.reshape(2, widths[0], blocks, LANES).transpose(1, 2, 0, 3).reshape(-1, LANES)
    ind_taps = ind_kernel.transpose(1, 0, 2)
    vmem = pl.BlockSpec(memory_space=pltpu.VMEM)
    outgoing, wanted = pl.pallas_call(
        lambda *refs: conv_kernel(reach, widths, *refs),
        out_shape=(pltpu.VMEM((tiles, SUB, LANES), jnp.float32),
                   pltpu.VMEM((3, SUB, cell_u.shape[2]), jnp.int32)),
        in_specs=[pl.BlockSpec(memory_space=pltpu.HBM)] * 8,
        out_specs=(vmem, vmem),
        scratch_shapes=[
            pltpu.VMEM(ind_rows.shape, jnp.bfloat16),
            pltpu.VMEM(col_frames.shape, jnp.bfloat16),
            pltpu.VMEM(ind_taps.shape, jnp.bfloat16),
            pltpu.VMEM(col_kernel.shape, jnp.bfloat16),
            pltpu.VMEM((3,) + cell_u.shape[0:], jnp.int32),
            pltpu.SMEM(tile_counts.shape, jnp.int32),
            pltpu.SemaphoreType.DMA((8,)),
            pltpu.VMEM((3, offsets * bins, 2 * window), jnp.bfloat16),
            pltpu.VMEM((3, GROUP * blocks, 2 * window), jnp.bfloat16),
        ],
        name="deconvolve",
    )(ind_rows, col_frames, ind_taps, col_kernel, cell_u, cell_v, cell_w, tile_counts)
    arrived = lax.all_to_all(outgoing, "wire", split_axis=0, concat_axis=0, tiled=True)
    return pl.pallas_call(
        lambda *refs: cell_kernel(reach, widths, *refs),
        out_shape=jax.ShapeDtypeStruct((1, 1, SUB, cell_u.shape[2]), jnp.float32),
        in_specs=[vmem] * 2,
        out_specs=vmem,
        name="cells",
        compiler_params=pltpu.CompilerParams(vmem_limit_bytes=4 << 20),
    )(arrived, wanted)


def solution(mesh):
    return jax.shard_map(
        on_device,
        mesh=mesh,
        in_specs=(
            P("apa", None, "wire", None),
            P("apa", "wire", None),
            P(),
            P(),
            P("apa", "wire", None),
            P("apa", "wire", None),
            P("apa", "wire", None),
            P("apa", "wire"),
        ),
        out_specs=P("apa", "wire", None, None),
        check_vma=False,
    )
```

time: 28.5 us -> 27.6 us (0.968)
  blocking collectives: 0 us -> 23.4 us
  starting transfers between devices: 13.3 us -> 0 us
  waiting for transfers between devices: 9.8 us -> 0 us
  Pallas kernels: 4.45 us -> 3.36 us
    all_to_all x0 -> x1, blocking collectives: none -> 23.4 us  [on_device(): lax.all_to_all(outgoing, 'wire', split_axis=0, concat_axis=0, tiled=True)]
    all_to_all x1 -> x0, starting transfers between devices: 13.3 us -> none  [on_device(): lax.all_to_all(outgoing, 'wire', split_axis=0, concat_axis=0, tiled=True)]
    all_to_all x1 -> x0, waiting for transfers between devices: 9.8 us -> none  [on_device(): lax.all_to_all(outgoing, 'wire', split_axis=0, concat_axis=0, tiled=True)]
    pallas_call x1, Pallas kernels: 3.26 us -> 2.45 us  [on_device(): pl.pallas_call(lambda *refs: conv_kernel(reach, widths, *refs), out_shape...]
    pallas_call x1, Pallas kernels: 1.2 us -> 0.91 us  [on_device(): pl.pallas_call(lambda *refs: cell_kernel(reach, widths, *refs), out_shape...]
  transfers between devices with their start and end apart: 1 -> 0, of which waited for: 1 -> 0; matrix products, arithmetic and copies ran while one was open for 0% -> 0% of each run, Pallas kernels for 0% -> 0%
where the time goes in v3:
time: 27.6 us; the launch traced here: 27.4 us
  blocking collectives  23.4 us (85%)
  Pallas kernels  3.36 us (12%)
  between operations  0.66 us (2%)
    all_to_all x1, blocking collectives, on_device(): lax.all_to_all(outgoing, 'wire', split_axis=0, concat_axis=0, tiled=True)  23.4 us
    pallas_call x1, Pallas kernels, on_device(): pl.pallas_call(lambda *refs: conv_kernel(reach, widths, *refs), out_shape...  2.45 us
    pallas_call x1, Pallas kernels, on_device(): pl.pallas_call(lambda *refs: cell_kernel(reach, widths, *refs), out_shape...  0.91 us

profile of v3, /device:TPU:56, one launch (start us, length us, event | category | flops | bytes accessed | tf_op | source)
XLA Modules:
  0.0 27.4 jit_solution(1088107500239434660)
XLA Ops:
  0.7 2.5 %deconvolve.1 = (f32[32,8,128]{2,1,0:T(8,128)S(1)}, s32[3,8,512]{2,1,0:T(8,128)S(1)}) custom-call(bf16[400,128]{1,0:T(8,128)(2,1)} %bitcast.6, bf16[1,30,1024]{2,1,0:T(8,128)(2,1)} %refs_1_.1, bf16[11,2,256]{2,1,0:T(2,128)(2,1)} %bitcast.7, bf16[11,256]{1,0:T(8,128)(2,1)} %refs_3_.1, s32[1,1,512]{2,1,0:T(1,128)} %refs_4_.1, s32[1,1,512]{2,1,0:T(1,128)} %refs_5_.1, ...), custom_call_target="tpu_custom_call" | custom-call | tf_op jit(solution)/shard_map/deconvolve/pallas_call | solution.py:213
  3.1 23.4 %all_to_all.5.refs_0_ = f32[32,8,128]{2,1,0:T(8,128)S(1)} all-to-all(f32[32,8,128]{2,1,0:T(8,128)S(1)} %get-tuple-element.7), channel_id=1, replica_groups=mesh['apa'=16,'wire'=32] {'wire'}, dimensions={0} | all-to-all | bytes 262144 | tf_op jit(solution)/shard_map/all_to_all | solution.py:232
  26.5 0.9 %cells.1 = f32[1,1,8,512]{3,2,1,0:T(8,128)} custom-call(f32[32,8,128]{2,1,0:T(8,128)S(1)} %all_to_all.5.refs_0_, s32[3,8,512]{2,1,0:T(8,128)S(1)} %get-tuple-element.8.refs_1_), custom_call_target="tpu_custom_call" | custom-call | tf_op jit(solution)/shard_map/cells/pallas_call | solution.py:233

commit v4 on v3

--- a/solution.py
+++ b/solution.py
@@ -23,7 +23,7 @@
 
 
 def conv_kernel(reach, widths, ind_hbm, col_hbm, indk_hbm, colk_hbm, u_hbm, v_hbm, w_hbm, count_hbm,
-                out, where_out, indf, colf, indk, colk, cells, count, sems, toep, wide):
+                out, where_out, indf, colf, indk, colk, cells, count, sems, toep, wide, moved):
     copies = [pltpu.make_async_copy(source, target, sems.at[i]) for i, (source, target) in enumerate((
         (indk_hbm, indk), (colk_hbm, colk), (ind_hbm, indf), (col_hbm, colf),
         (u_hbm, cells.at[0]), (v_hbm, cells.at[1]), (w_hbm, cells.at[2]), (count_hbm, count)))]
@@ -48,15 +48,20 @@
     wanted = ((place & (GROUP - 1)) * blocks + place // GROUP) * 2
     pick = [(source == wanted + p).astype(jnp.float32).astype(jnp.bfloat16) for p in range(2)]
 
-    for copy in copies:
-        copy.wait()
+    copies[0].wait()
+    copies[1].wait()
 
     both = indk[...]
     rows_of = [jnp.dot(k, fold, preferred_element_type=jnp.float32)
                for k in (both[:, 0, :], both[:, 1, :], colk[...])]
 
-    sums = []
-    for plane in range(3):
+    mine = lax.axis_index("wire") & (TURN - 1)
+    group = (lanes // GROUP - mine) & (TURN - 1)
+    in_group = [group == i for i in range(TURN)]
+    slot = lanes & (GROUP - 1)
+    per_half = LANES // GROUP
+
+    def spread(plane):
         width = widths[plane]
         blank = jnp.zeros((GROUP, LANES), jnp.bfloat16)
         if plane < 2:
@@ -72,6 +77,8 @@
                 piece = tiles[block + i]
                 wide[plane, GROUP * block:GROUP * (block + 1), LANES * i:LANES * (i + 1)] = piece
                 wide[plane, GROUP * block:GROUP * (block + 1), window + LANES * i:window + LANES * (i + 1)] = piece
+
+    def toeplitz(plane):
         for offset in range(offsets):
             row = rows_of[plane][offset:offset + 1, :]
             flat = [jnp.broadcast_to(row[:, LANES * i:LANES * (i + 1)], (SUB, LANES)) for i in range(pieces)]
@@ -90,30 +97,17 @@
                     low = (exact - high.astype(jnp.float32)).astype(jnp.bfloat16)
                     toep[plane, at_row:at_row + 16, LANES * i:LANES * (i + 1)] = high
                     toep[plane, at_row:at_row + 16, window + LANES * i:window + LANES * (i + 1)] = low
+
+    def multiply(plane):
         grid = lax.dot_general(
             toep[plane], wide[plane], (((1,), (1,)), ((), ())),
             preferred_element_type=jnp.float32)
-        sums.append(grid)
-
-    for plane in range(3):
-        width = widths[plane]
-        for chunk in range(cells.shape[3] // LANES):
-            span = slice(chunk * LANES, (chunk + 1) * LANES)
-            wire = jnp.broadcast_to(cells[plane, 0, 0:1, span], (SUB, LANES))
-            owner = (wire * ((1 << 18) // width + 1)) >> 18
-            spot = wire - owner * width + ((owner + plane) & (TURN - 1)) * GROUP
-            spot = spot + (owner // TURN) * LANES
-            live = lanes + chunk * LANES < count[0, 0]
-            where_out[plane, :, span] = jnp.where(live, spot, -1)
-
-    turn = (lax.axis_index("wire") & (TURN - 1)) * GROUP
-    spots = (lanes - turn) & (LANES - 1)
-    slot = lanes & (GROUP - 1)
-    per_half = LANES // GROUP
-    for half in range(blocks // per_half):
-        for part in range(bins // SUB):
-            gathered = []
-            for plane in range(3):
+        return grid
+
+
+    def shift_add(plane, grid):
+        for half in range(blocks // per_half):
+            for part in range(bins // SUB):
                 width = widths[plane]
                 spare = GROUP - width
 
@@ -121,7 +115,7 @@
                     acc = None
                     for shift in range(first, last + 1):
                         at_row = (reach - shift) * bins + part * SUB
-                        piece = sums[plane][at_row:at_row + SUB, LANES * half:LANES * (half + 1)]
+                        piece = grid[at_row:at_row + SUB, LANES * half:LANES * (half + 1)]
                         piece = piece if shift == 0 else pltpu.roll(piece, shift % LANES, 1)
                         acc = piece if acc is None else acc + piece
                     return acc
@@ -136,24 +130,59 @@
                     near, far = run(-spare, -1), run(-reach, -spare - 1)
                     main = main + near + jnp.where(slot < GROUP - reach, far, 0.0)
                     before = jnp.where(slot >= width, near, 0.0) + far
-                extra = (TURN - 1) * GROUP + reach * plane
-                gathered += [(main, 0, GROUP * plane, width),
-                             (after, width, extra + RIGHT, reach),
-                             (before, -reach, extra + LEFT, reach)]
+                main = pltpu.roll(main, ((plane + mine) & (TURN - 1)) * GROUP, 1)
+                for i, value in enumerate((main, after, before)):
+                    moved[plane, i, half * (bins // SUB) + part] = value
+
+    for copy in copies[2:]:
+        copy.wait()
+    grids = []
+    for plane in range(3):
+        spread(plane)
+        toeplitz(plane)
+        grids.append(multiply(plane))
+    for plane in range(3):
+        shift_add(plane, grids[plane])
+
+    stand = lax.axis_index("wire") // (bins // SUB) & (TURN - 1)
+    for plane in range(3):
+        width = widths[plane]
+        for chunk in range(cells.shape[3] // LANES):
+            span = slice(chunk * LANES, (chunk + 1) * LANES)
+            wire = jnp.broadcast_to(cells[plane, 0, 0:1, span], (SUB, LANES))
+            owner = (wire * ((1 << 18) // width + 1)) >> 18
+            spot = wire - owner * width + ((owner + plane + stand) & (TURN - 1)) * GROUP
+            spot = spot + (owner // TURN) * LANES
+            live = lanes + chunk * LANES < count[0, 0]
+            where_out[plane, :, span] = jnp.where(live, spot, -1)
+
+
+    edge = ((TURN - 1 + mine) & (TURN - 1)) * GROUP
+    for half in range(blocks // per_half):
+        for part in range(bins // SUB):
+            step = half * (bins // SUB) + part
+            turned = [moved[plane, 0, step] for plane in range(3)]
+            edges, halo = [], None
+            for plane in range(3):
+                edges += [(RIGHT + reach * plane, widths[plane], moved[plane, 1, step]),
+                          (LEFT + reach * plane, -reach, moved[plane, 2, step])]
+            for target, begin, acc in sorted(edges, key=lambda item: item[0]):
+                placed = pltpu.roll(acc, (edge + (target - begin) % LANES) & (LANES - 1), 1)
+                halo = placed if halo is None else jnp.where(slot >= target, placed, halo)
+            turned.append(halo)
             for spot in range(per_half):
                 tile = (half * per_half + spot) * (bins // SUB) + part
-                result = jnp.zeros((SUB, LANES), jnp.float32)
-                for acc, begin, target, size in gathered:
-                    amount = (turn + (target - begin - GROUP * spot) % LANES) & (LANES - 1)
-                    placed = pltpu.roll(acc, amount, 1)
-                    result = jnp.where(between(spots, target, target + size), placed, result)
+                result = turned[0]
+                for plane in range(1, TURN):
+                    result = jnp.where(in_group[(spot + plane) % TURN], turned[plane], result)
                 out[tile] = result
 
 
 def cell_kernel(reach, widths, table, wanted, out):
     sources = table.shape[0]
     lanes = lane_iota()
-    group = lanes // GROUP
+    stand = lax.axis_index("wire") // (LANES // REBIN // SUB) & (TURN - 1)
+    group = (lanes // GROUP - stand) & (TURN - 1)
     slot = lanes & (GROUP - 1)
     zero = jnp.zeros((SUB, LANES), jnp.float32)
 
@@ -178,8 +207,8 @@
         first = slot < reach
         last = between(slot, width - reach, width)
         index = jnp.where(
-            first, ((group - plane + 2) & (TURN - 1)) * GROUP + RIGHT + reach * plane + slot,
-            ((group - plane) & (TURN - 1)) * GROUP + LEFT + reach * plane + slot - (width - reach))
+            first, ((group - plane + 2 + stand) & (TURN - 1)) * GROUP + RIGHT + reach * plane + slot,
+            ((group - plane + stand) & (TURN - 1)) * GROUP + LEFT + reach * plane + slot - (width - reach))
         index = jnp.where(first | last, index, lanes)
         full.append([joined(stage, plane) + jnp.where(
             first | last, jnp.take_along_axis(mixed[stage], index, axis=1), 0.0) for stage in range(stages)])
@@ -226,6 +255,7 @@
             pltpu.SemaphoreType.DMA((8,)),
             pltpu.VMEM((3, offsets * bins, 2 * window), jnp.bfloat16),
             pltpu.VMEM((3, GROUP * blocks, 2 * window), jnp.bfloat16),
+            pltpu.VMEM((3, 3, tiles // TURN, SUB, LANES), jnp.float32),
         ],
         name="deconvolve",
     )(ind_rows, col_frames, ind_taps, col_kernel, cell_u, cell_v, cell_w, tile_counts)

time: 27.6 us -> 27.4 us (level)
  no operation moved by 1% of the time
where the time goes in v4:
time: 27.4 us; the launch traced here: 27.2 us
  blocking collectives  23.5 us (86%)
  Pallas kernels  3.1 us (11%)
  between operations  0.66 us (2%)
    all_to_all x1, blocking collectives, on_device(): lax.all_to_all(outgoing, 'wire', split_axis=0, concat_axis=0, tiled=True)  23.5 us
    pallas_call x1, Pallas kernels, on_device(): pl.pallas_call(lambda *refs: conv_kernel(reach, widths, *refs), out_shape...  2.19 us
    pallas_call x1, Pallas kernels, on_device(): pl.pallas_call(lambda *refs: cell_kernel(reach, widths, *refs), out_shape...  0.92 us

profile of v4, /device:TPU:56, one launch (start us, length us, event | category | flops | bytes accessed | tf_op | source)
XLA Modules:
  0.0 27.2 jit_solution(10182075266039689532)
XLA Ops:
  0.7 2.2 %deconvolve.1 = (f32[32,8,128]{2,1,0:T(8,128)S(1)}, s32[3,8,512]{2,1,0:T(8,128)S(1)}) custom-call(bf16[400,128]{1,0:T(8,128)(2,1)} %bitcast.6, bf16[1,30,1024]{2,1,0:T(8,128)(2,1)} %refs_1_.1, bf16[11,2,256]{2,1,0:T(2,128)(2,1)} %bitcast.7, bf16[11,256]{1,0:T(8,128)(2,1)} %refs_3_.1, s32[1,1,512]{2,1,0:T(1,128)} %refs_4_.1, s32[1,1,512]{2,1,0:T(1,128)} %refs_5_.1, ...), custom_call_target="tpu_custom_call" | custom-call | tf_op jit(solution)/shard_map/deconvolve/pallas_call | solution.py:242
  2.8 23.5 %all_to_all.5.refs_0_ = f32[32,8,128]{2,1,0:T(8,128)S(1)} all-to-all(f32[32,8,128]{2,1,0:T(8,128)S(1)} %get-tuple-element.7), channel_id=1, replica_groups=mesh['apa'=16,'wire'=32] {'wire'}, dimensions={0} | all-to-all | bytes 262144 | tf_op jit(solution)/shard_map/all_to_all | solution.py:262
  26.3 0.9 %cells.1 = f32[1,1,8,512]{3,2,1,0:T(8,128)} custom-call(f32[32,8,128]{2,1,0:T(8,128)S(1)} %all_to_all.5.refs_0_, s32[3,8,512]{2,1,0:T(8,128)S(1)} %get-tuple-element.8.refs_1_), custom_call_target="tpu_custom_call" | custom-call | tf_op jit(solution)/shard_map/cells/pallas_call | solution.py:263

commit v5 on v4

--- a/solution.py
+++ b/solution.py
@@ -8,6 +8,7 @@
 LANES = 128
 SUB = 8
 REBIN = 4
+HALF = 16
 GROUP = 32
 TURN = LANES // GROUP
 RIGHT = 0
@@ -42,11 +43,11 @@
     total = (lax.broadcasted_iota(jnp.int32, (taps, window), 0)
              + lax.broadcasted_iota(jnp.int32, (taps, window), 1))
     fold = between(total, taps, taps + REBIN).astype(jnp.float32).astype(jnp.bfloat16)
-    height = GROUP * blocks
-    place = lax.broadcasted_iota(jnp.int32, (height, indf.shape[0]), 0)
-    source = lax.broadcasted_iota(jnp.int32, (height, indf.shape[0]), 1)
-    wanted = ((place & (GROUP - 1)) * blocks + place // GROUP) * 2
-    pick = [(source == wanted + p).astype(jnp.float32).astype(jnp.bfloat16) for p in range(2)]
+    part_rows = 2 * blocks * HALF
+    place = lax.broadcasted_iota(jnp.int32, (part_rows, part_rows), 0)
+    source = lax.broadcasted_iota(jnp.int32, (part_rows, part_rows), 1)
+    wanted = (place & (HALF - 1)) * (2 * blocks) + (place // HALF & (blocks - 1)) * 2 + place // (part_rows // 2)
+    pick = (source == wanted).astype(jnp.float32).astype(jnp.bfloat16)
 
     copies[0].wait()
     copies[1].wait()
@@ -61,22 +62,22 @@
     slot = lanes & (GROUP - 1)
     per_half = LANES // GROUP
 
-    def spread(plane):
+    def spread(plane, rows):
         width = widths[plane]
-        blank = jnp.zeros((GROUP, LANES), jnp.bfloat16)
-        if plane < 2:
-            ordered = jnp.dot(pick[plane], indf[...], preferred_element_type=jnp.float32).astype(jnp.bfloat16)
-            tiles = [ordered[GROUP * i:GROUP * (i + 1)] for i in range(blocks)]
-        else:
-            spare = jnp.zeros((GROUP - width, ticks), jnp.bfloat16)
-            padded = jnp.concatenate([colf[0], spare], axis=0)
-            tiles = [padded[:, LANES * i:LANES * (i + 1)] for i in range(blocks)]
-        tiles = [blank] * history + tiles
-        for block in range(blocks):
-            for i in range(pieces):
-                piece = tiles[block + i]
-                wide[plane, GROUP * block:GROUP * (block + 1), LANES * i:LANES * (i + 1)] = piece
-                wide[plane, GROUP * block:GROUP * (block + 1), window + LANES * i:window + LANES * (i + 1)] = piece
+        blank = jnp.zeros((HALF, LANES), jnp.bfloat16)
+        for part in range(GROUP // HALF):
+            if plane < 2:
+                at = plane * blocks
+                tiles = [rows[part][HALF * (at + i):HALF * (at + i + 1)] for i in range(blocks)]
+            else:
+                count = min(HALF, width - HALF * part)
+                mine = colf[0, HALF * part:HALF * part + count, :]
+                if count < HALF:
+                    mine = jnp.concatenate([mine, jnp.zeros((HALF - count, ticks), jnp.bfloat16)], axis=0)
+                tiles = [mine[:, LANES * i:LANES * (i + 1)] for i in range(blocks)]
+            for block, piece in enumerate([blank] * history + tiles):
+                row = GROUP * block + HALF * part
+                wide[plane, row:row + HALF, :] = piece
 
     def toeplitz(plane):
         for offset in range(offsets):
@@ -99,8 +100,9 @@
                     toep[plane, at_row:at_row + 16, window + LANES * i:window + LANES * (i + 1)] = low
 
     def multiply(plane):
+        seen = [wide[plane, GROUP * i:GROUP * (i + blocks), :] for i in range(pieces)]
         grid = lax.dot_general(
-            toep[plane], wide[plane], (((1,), (1,)), ((), ())),
+            toep[plane], jnp.concatenate(seen + seen, axis=1), (((1,), (1,)), ((), ())),
             preferred_element_type=jnp.float32)
         return grid
 
@@ -136,10 +138,14 @@
 
     for copy in copies[2:]:
         copy.wait()
+    rows = [jnp.dot(pick[:, :min(part_rows, indf.shape[0] - at)], indf[at:min(at + part_rows, indf.shape[0]), :],
+                    preferred_element_type=jnp.float32).astype(jnp.bfloat16)
+            for at in range(0, indf.shape[0], part_rows)]
     grids = []
     for plane in range(3):
-        spread(plane)
+        spread(plane, rows)
         toeplitz(plane)
+    for plane in range(3):
         grids.append(multiply(plane))
     for plane in range(3):
         shift_add(plane, grids[plane])
@@ -254,7 +260,7 @@
             pltpu.SMEM(tile_counts.shape, jnp.int32),
             pltpu.SemaphoreType.DMA((8,)),
             pltpu.VMEM((3, offsets * bins, 2 * window), jnp.bfloat16),
-            pltpu.VMEM((3, GROUP * blocks, 2 * window), jnp.bfloat16),
+            pltpu.VMEM((3, GROUP * (blocks + taps // LANES), LANES), jnp.bfloat16),
             pltpu.VMEM((3, 3, tiles // TURN, SUB, LANES), jnp.float32),
         ],
         name="deconvolve",

time: 27.4 us -> 27.3 us (level)
  no operation moved by 1% of the time
where the time goes in v5:
time: 27.3 us; the launch traced here: 27 us
  blocking collectives  23.4 us (86%)
  Pallas kernels  2.97 us (11%)
  between operations  0.66 us (2%)
    all_to_all x1, blocking collectives, on_device(): lax.all_to_all(outgoing, 'wire', split_axis=0, concat_axis=0, tiled=True)  23.4 us
    pallas_call x1, Pallas kernels, on_device(): pl.pallas_call(lambda *refs: conv_kernel(reach, widths, *refs), out_shape...  2.05 us
    pallas_call x1, Pallas kernels, on_device(): pl.pallas_call(lambda *refs: cell_kernel(reach, widths, *refs), out_shape...  0.92 us

profile of v5, /device:TPU:56, one launch (start us, length us, event | category | flops | bytes accessed | tf_op | source)
XLA Modules:
  0.0 27.0 jit_solution(10329406965026597140)
XLA Ops:
  0.7 2.0 %deconvolve.1 = (f32[32,8,128]{2,1,0:T(8,128)S(1)}, s32[3,8,512]{2,1,0:T(8,128)S(1)}) custom-call(bf16[400,128]{1,0:T(8,128)(2,1)} %bitcast.6, bf16[1,30,1024]{2,1,0:T(8,128)(2,1)} %refs_1_.1, bf16[11,2,256]{2,1,0:T(2,128)(2,1)} %bitcast.7, bf16[11,256]{1,0:T(8,128)(2,1)} %refs_3_.1, s32[1,1,512]{2,1,0:T(1,128)} %refs_4_.1, s32[1,1,512]{2,1,0:T(1,128)} %refs_5_.1, ...), custom_call_target="tpu_custom_call" | custom-call | tf_op jit(solution)/shard_map/deconvolve/pallas_call | solution.py:248
  2.7 23.4 %all_to_all.5.refs_0_ = f32[32,8,128]{2,1,0:T(8,128)S(1)} all-to-all(f32[32,8,128]{2,1,0:T(8,128)S(1)} %get-tuple-element.7), channel_id=1, replica_groups=mesh['apa'=16,'wire'=32] {'wire'}, dimensions={0} | all-to-all | bytes 262144 | tf_op jit(solution)/shard_map/all_to_all | solution.py:268
  26.1 0.9 %cells.1 = f32[1,1,8,512]{3,2,1,0:T(8,128)} custom-call(f32[32,8,128]{2,1,0:T(8,128)S(1)} %all_to_all.5.refs_0_, s32[3,8,512]{2,1,0:T(8,128)S(1)} %get-tuple-element.8.refs_1_), custom_call_target="tpu_custom_call" | custom-call | tf_op jit(solution)/shard_map/cells/pallas_call | solution.py:269

commit v6 on v5

--- a/solution.py
+++ b/solution.py
@@ -24,9 +24,9 @@
 
 
 def conv_kernel(reach, widths, ind_hbm, col_hbm, indk_hbm, colk_hbm, u_hbm, v_hbm, w_hbm, count_hbm,
-                out, where_out, indf, colf, indk, colk, cells, count, sems, toep, wide, moved):
+                out, where_out, extras, indf, colf, indk, colk, cells, count, sems, toep, wide, filters, moved):
     copies = [pltpu.make_async_copy(source, target, sems.at[i]) for i, (source, target) in enumerate((
-        (indk_hbm, indk), (colk_hbm, colk), (ind_hbm, indf), (col_hbm, colf),
+        (indk_hbm, indk), (colk_hbm, colk), (ind_hbm.at[0:256], indf.at[0:256]), (ind_hbm.at[256:400], indf.at[256:400]), (col_hbm.at[:, :, 0:512], colf.at[:, :, 0:512]), (col_hbm.at[:, :, 512:1024], colf.at[:, :, 512:1024]),
         (u_hbm, cells.at[0]), (v_hbm, cells.at[1]), (w_hbm, cells.at[2]), (count_hbm, count)))]
     for copy in copies:
         copy.start()
@@ -40,8 +40,9 @@
     lanes = lane_iota()
     subs = lax.broadcasted_iota(jnp.int32, (SUB, LANES), 0)
 
-    total = (lax.broadcasted_iota(jnp.int32, (taps, window), 0)
-             + lax.broadcasted_iota(jnp.int32, (taps, window), 1))
+    tap = lax.broadcasted_iota(jnp.int32, (taps, window), 0)
+    column = lax.broadcasted_iota(jnp.int32, (taps, window), 1)
+    total = tap + jnp.where(column < taps, column, taps + (column & (REBIN - 1)))
     fold = between(total, taps, taps + REBIN).astype(jnp.float32).astype(jnp.bfloat16)
     part_rows = 2 * blocks * HALF
     place = lax.broadcasted_iota(jnp.int32, (part_rows, part_rows), 0)
@@ -49,12 +50,27 @@
     wanted = (place & (HALF - 1)) * (2 * blocks) + (place // HALF & (blocks - 1)) * 2 + place // (part_rows // 2)
     pick = (source == wanted).astype(jnp.float32).astype(jnp.bfloat16)
 
+    stand = lax.axis_index("wire") // (bins // SUB) & (TURN - 1)
+    group = (lanes // GROUP - stand) & (TURN - 1)
+    slot = lanes & (GROUP - 1)
+    for plane in range(3):
+        width = widths[plane]
+        first = slot < reach
+        last = between(slot, width - reach, width)
+        index = jnp.where(
+            first, ((group - plane + 2 + stand) & (TURN - 1)) * GROUP + RIGHT + reach * plane + slot,
+            ((group - plane + stand) & (TURN - 1)) * GROUP + LEFT + reach * plane + slot - (width - reach))
+        extras[plane] = jnp.where(first | last, index, -1)
+
+    filters[...] = jnp.zeros_like(filters)
     copies[0].wait()
     copies[1].wait()
 
     both = indk[...]
-    rows_of = [jnp.dot(k, fold, preferred_element_type=jnp.float32)
-               for k in (both[:, 0, :], both[:, 1, :], colk[...])]
+    for plane, k in enumerate((both[:, 0, :], both[:, 1, :], colk[...])):
+        filters[16 * plane:16 * plane + offsets, :] = k
+    all_rows = jnp.dot(filters[...], fold, preferred_element_type=jnp.float32)
+    rows_of = [all_rows[16 * plane:16 * plane + offsets] for plane in range(3)]
 
     mine = lax.axis_index("wire") & (TURN - 1)
     group = (lanes // GROUP - mine) & (TURN - 1)
@@ -86,10 +102,13 @@
             made = []
             for part in range(bins // SUB):
                 base = part * SUB * REBIN
-                turned = [pltpu.roll(piece, base, 1, stride=REBIN, stride_axis=0) for piece in flat]
-                keep = lanes >= base + REBIN * subs
-                before = [jnp.zeros_like(turned[0])] + turned[:-1]
-                made.append([jnp.where(keep, a, b) for a, b in zip(turned, before)])
+                shift = base + REBIN * subs
+                turned = [pltpu.roll(piece, base, 1, stride=REBIN, stride_axis=0) for piece in flat[:-1]]
+                own = jnp.where(lanes < shift + REBIN, flat[-1], 0.0)
+                after = turned[1:] + [own]
+                before = turned
+                made.append([jnp.where(lanes >= shift, turned[0], 0.0)]
+                            + [jnp.where(lanes >= shift, a, b) for a, b in zip(after, before)])
             for pair in range(0, len(made), 2):
                 at_row = offset * bins + pair * SUB
                 for i in range(pieces):
@@ -184,7 +203,7 @@
                 out[tile] = result
 
 
-def cell_kernel(reach, widths, table, wanted, out):
+def cell_kernel(table, wanted, extras, out):
     sources = table.shape[0]
     lanes = lane_iota()
     stand = lax.axis_index("wire") // (LANES // REBIN // SUB) & (TURN - 1)
@@ -209,15 +228,11 @@
         mixed.append(jnp.where(late, halos[stage + 1] if stage + 1 < stages else zero, made))
     full = []
     for plane in range(3):
-        width = widths[plane]
-        first = slot < reach
-        last = between(slot, width - reach, width)
-        index = jnp.where(
-            first, ((group - plane + 2 + stand) & (TURN - 1)) * GROUP + RIGHT + reach * plane + slot,
-            ((group - plane + stand) & (TURN - 1)) * GROUP + LEFT + reach * plane + slot - (width - reach))
-        index = jnp.where(first | last, index, lanes)
+        index = extras[plane]
+        added = index >= 0
+        index = index & (LANES - 1)
         full.append([joined(stage, plane) + jnp.where(
-            first | last, jnp.take_along_axis(mixed[stage], index, axis=1), 0.0) for stage in range(stages)])
+            added, jnp.take_along_axis(mixed[stage], index, axis=1), 0.0) for stage in range(stages)])
 
     for chunk in range(wanted.shape[2] // LANES):
         span = slice(chunk * LANES, (chunk + 1) * LANES)
@@ -245,12 +260,13 @@
     ind_rows = ind_frames.reshape(2, widths[0], blocks, LANES).transpose(1, 2, 0, 3).reshape(-1, LANES)
     ind_taps = ind_kernel.transpose(1, 0, 2)
     vmem = pl.BlockSpec(memory_space=pltpu.VMEM)
-    outgoing, wanted = pl.pallas_call(
+    outgoing, wanted, extras = pl.pallas_call(
         lambda *refs: conv_kernel(reach, widths, *refs),
         out_shape=(pltpu.VMEM((tiles, SUB, LANES), jnp.float32),
-                   pltpu.VMEM((3, SUB, cell_u.shape[2]), jnp.int32)),
+                   pltpu.VMEM((3, SUB, cell_u.shape[2]), jnp.int32),
+                   pltpu.VMEM((3, SUB, LANES), jnp.int32)),
         in_specs=[pl.BlockSpec(memory_space=pltpu.HBM)] * 8,
-        out_specs=(vmem, vmem),
+        out_specs=(vmem, vmem, vmem),
         scratch_shapes=[
             pltpu.VMEM(ind_rows.shape, jnp.bfloat16),
             pltpu.VMEM(col_frames.shape, jnp.bfloat16),
@@ -258,22 +274,23 @@
             pltpu.VMEM(col_kernel.shape, jnp.bfloat16),
             pltpu.VMEM((3,) + cell_u.shape[0:], jnp.int32),
             pltpu.SMEM(tile_counts.shape, jnp.int32),
-            pltpu.SemaphoreType.DMA((8,)),
+            pltpu.SemaphoreType.DMA((10,)),
             pltpu.VMEM((3, offsets * bins, 2 * window), jnp.bfloat16),
             pltpu.VMEM((3, GROUP * (blocks + taps // LANES), LANES), jnp.bfloat16),
+            pltpu.VMEM((3 * 16, taps), jnp.bfloat16),
             pltpu.VMEM((3, 3, tiles // TURN, SUB, LANES), jnp.float32),
         ],
         name="deconvolve",
     )(ind_rows, col_frames, ind_taps, col_kernel, cell_u, cell_v, cell_w, tile_counts)
     arrived = lax.all_to_all(outgoing, "wire", split_axis=0, concat_axis=0, tiled=True)
     return pl.pallas_call(
-        lambda *refs: cell_kernel(reach, widths, *refs),
+        cell_kernel,
         out_shape=jax.ShapeDtypeStruct((1, 1, SUB, cell_u.shape[2]), jnp.float32),
-        in_specs=[vmem] * 2,
+        in_specs=[vmem] * 3,
         out_specs=vmem,
         name="cells",
         compiler_params=pltpu.CompilerParams(vmem_limit_bytes=4 << 20),
-    )(arrived, wanted)
+    )(arrived, wanted, extras)
 
 
 def solution(mesh):

time: 27.3 us -> 27.2 us (level)
  no operation moved by 1% of the time
where the time goes in v6:
time: 27.2 us; the launch traced here: 27 us
  blocking collectives  23.4 us (86%)
  Pallas kernels  2.93 us (11%)
  between operations  0.66 us (2%)
    all_to_all x1, blocking collectives, on_device(): lax.all_to_all(outgoing, 'wire', split_axis=0, concat_axis=0, tiled=True)  23.4 us
    pallas_call x1, Pallas kernels, on_device(): pl.pallas_call(lambda *refs: conv_kernel(reach, widths, *refs), out_shape...  2.02 us
    pallas_call x1, Pallas kernels, on_device(): pl.pallas_call(cell_kernel, out_shape=jax.ShapeDtypeStruct((1, 1, SUB, ce...  0.91 us

profile of v6, /device:TPU:56, one launch (start us, length us, event | category | flops | bytes accessed | tf_op | source)
XLA Modules:
  0.0 27.0 jit_solution(12988806257940513428)
XLA Ops:
  0.7 2.0 %deconvolve.1 = (f32[32,8,128]{2,1,0:T(8,128)S(1)}, s32[3,8,512]{2,1,0:T(8,128)S(1)}, s32[3,8,128]{2,1,0:T(8,128)S(1)}) custom-call(bf16[400,128]{1,0:T(8,128)(2,1)} %bitcast.6, bf16[1,30,1024]{2,1,0:T(8,128)(2,1)} %refs_1_.1, bf16[11,2,256]{2,1,0:T(2,128)(2,1)} %bitcast.7, bf16[11,256]{1,0:T(8,128)(2,1)} %refs_3_.1, s32[1,1,512]{2,1,0:T(1,128)} %refs_4_.1, ...), custom_call_target="tpu_custom_call" | custom-call | tf_op jit(solution)/shard_map/deconvolve/pallas_call | solution.py:263
  2.7 23.4 %all_to_all.5.table = f32[32,8,128]{2,1,0:T(8,128)S(1)} all-to-all(f32[32,8,128]{2,1,0:T(8,128)S(1)} %get-tuple-element.8), channel_id=1, replica_groups=mesh['apa'=16,'wire'=32] {'wire'}, dimensions={0} | all-to-all | bytes 262144 | tf_op jit(solution)/shard_map/all_to_all | solution.py:285
  26.1 0.9 %cells.1 = f32[1,1,8,512]{3,2,1,0:T(8,128)} custom-call(f32[32,8,128]{2,1,0:T(8,128)S(1)} %all_to_all.5.table, s32[3,8,512]{2,1,0:T(8,128)S(1)} %get-tuple-element.9.wanted, s32[3,8,128]{2,1,0:T(8,128)S(1)} %get-tuple-element.10.extras), custom_call_target="tpu_custom_call" | custom-call | tf_op jit(solution)/shard_map/cells/pallas_call | solution.py:286

commit v7 on v6

--- a/solution.py
+++ b/solution.py
@@ -24,7 +24,7 @@
 
 
 def conv_kernel(reach, widths, ind_hbm, col_hbm, indk_hbm, colk_hbm, u_hbm, v_hbm, w_hbm, count_hbm,
-                out, where_out, extras, indf, colf, indk, colk, cells, count, sems, toep, wide, filters, moved):
+                out, where_out, extras, indf, colf, indk, colk, cells, count, sems, toep, wide, filters, moved, sums):
     copies = [pltpu.make_async_copy(source, target, sems.at[i]) for i, (source, target) in enumerate((
         (indk_hbm, indk), (colk_hbm, colk), (ind_hbm.at[0:256], indf.at[0:256]), (ind_hbm.at[256:400], indf.at[256:400]), (col_hbm.at[:, :, 0:512], colf.at[:, :, 0:512]), (col_hbm.at[:, :, 512:1024], colf.at[:, :, 512:1024]),
         (u_hbm, cells.at[0]), (v_hbm, cells.at[1]), (w_hbm, cells.at[2]), (count_hbm, count)))]
@@ -120,13 +120,12 @@
 
     def multiply(plane):
         seen = [wide[plane, GROUP * i:GROUP * (i + blocks), :] for i in range(pieces)]
-        grid = lax.dot_general(
+        sums[plane] = lax.dot_general(
             toep[plane], jnp.concatenate(seen + seen, axis=1), (((1,), (1,)), ((), ())),
             preferred_element_type=jnp.float32)
-        return grid
-
-
-    def shift_add(plane, grid):
+
+
+    def shift_add(plane):
         for half in range(blocks // per_half):
             for part in range(bins // SUB):
                 width = widths[plane]
@@ -136,7 +135,7 @@
                     acc = None
                     for shift in range(first, last + 1):
                         at_row = (reach - shift) * bins + part * SUB
-                        piece = grid[at_row:at_row + SUB, LANES * half:LANES * (half + 1)]
+                        piece = sums[plane, at_row:at_row + SUB, LANES * half:LANES * (half + 1)]
                         piece = piece if shift == 0 else pltpu.roll(piece, shift % LANES, 1)
                         acc = piece if acc is None else acc + piece
                     return acc
@@ -160,14 +159,13 @@
     rows = [jnp.dot(pick[:, :min(part_rows, indf.shape[0] - at)], indf[at:min(at + part_rows, indf.shape[0]), :],
                     preferred_element_type=jnp.float32).astype(jnp.bfloat16)
             for at in range(0, indf.shape[0], part_rows)]
-    grids = []
     for plane in range(3):
         spread(plane, rows)
         toeplitz(plane)
     for plane in range(3):
-        grids.append(multiply(plane))
-    for plane in range(3):
-        shift_add(plane, grids[plane])
+        multiply(plane)
+    for plane in range(3):
+        shift_add(plane)
 
     stand = lax.axis_index("wire") // (bins // SUB) & (TURN - 1)
     for plane in range(3):
@@ -279,6 +277,7 @@
             pltpu.VMEM((3, GROUP * (blocks + taps // LANES), LANES), jnp.bfloat16),
             pltpu.VMEM((3 * 16, taps), jnp.bfloat16),
             pltpu.VMEM((3, 3, tiles // TURN, SUB, LANES), jnp.float32),
+            pltpu.VMEM((3, offsets * bins, GROUP * blocks), jnp.float32),
         ],
         name="deconvolve",
     )(ind_rows, col_frames, ind_taps, col_kernel, cell_u, cell_v, cell_w, tile_counts)

time: 27.2 us -> 27.2 us (level)
  no operation moved by 1% of the time
where the time goes in v7:
time: 27.2 us; the launch traced here: 27 us
  blocking collectives  23.4 us (86%)
  Pallas kernels  2.93 us (11%)
  between operations  0.66 us (2%)
    all_to_all x1, blocking collectives, on_device(): lax.all_to_all(outgoing, 'wire', split_axis=0, concat_axis=0, tiled=True)  23.4 us
    pallas_call x1, Pallas kernels, on_device(): pl.pallas_call(lambda *refs: conv_kernel(reach, widths, *refs), out_shape...  2.02 us
    pallas_call x1, Pallas kernels, on_device(): pl.pallas_call(cell_kernel, out_shape=jax.ShapeDtypeStruct((1, 1, SUB, ce...  0.91 us

profile of v7, /device:TPU:56, one launch (start us, length us, event | category | flops | bytes accessed | tf_op | source)
XLA Modules:
  0.0 27.0 jit_solution(12988806257940513428)
XLA Ops:
  0.7 2.0 %deconvolve.1 = (f32[32,8,128]{2,1,0:T(8,128)S(1)}, s32[3,8,512]{2,1,0:T(8,128)S(1)}, s32[3,8,128]{2,1,0:T(8,128)S(1)}) custom-call(bf16[400,128]{1,0:T(8,128)(2,1)} %bitcast.6, bf16[1,30,1024]{2,1,0:T(8,128)(2,1)} %refs_1_.1, bf16[11,2,256]{2,1,0:T(2,128)(2,1)} %bitcast.7, bf16[11,256]{1,0:T(8,128)(2,1)} %refs_3_.1, s32[1,1,512]{2,1,0:T(1,128)} %refs_4_.1, ...), custom_call_target="tpu_custom_call" | custom-call | tf_op jit(solution)/shard_map/deconvolve/pallas_call | solution.py:261
  2.7 23.4 %all_to_all.5.table = f32[32,8,128]{2,1,0:T(8,128)S(1)} all-to-all(f32[32,8,128]{2,1,0:T(8,128)S(1)} %get-tuple-element.8), channel_id=1, replica_groups=mesh['apa'=16,'wire'=32] {'wire'}, dimensions={0} | all-to-all | bytes 262144 | tf_op jit(solution)/shard_map/all_to_all | solution.py:284
  26.1 0.9 %cells.1 = f32[1,1,8,512]{3,2,1,0:T(8,128)} custom-call(f32[32,8,128]{2,1,0:T(8,128)S(1)} %all_to_all.5.table, s32[3,8,512]{2,1,0:T(8,128)S(1)} %get-tuple-element.9.wanted, s32[3,8,128]{2,1,0:T(8,128)S(1)} %get-tuple-element.10.extras), custom_call_target="tpu_custom_call" | custom-call | tf_op jit(solution)/shard_map/cells/pallas_call | solution.py:285
